TPU v7x, 32 devices: a whole 2x2x4 slice. The times are simulated.
32 devices in a mesh: gx: 4 (over y, x), gy: 4 (over z), ma: 2 (over core).
Axes of the slice: x: 2, y: 2, z: 4, core: 2. Of those that a mesh axis runs over, the one named last changes fastest.
Arguments:
- alpha_fields: bfloat16 [80, 2, 512, 512], P('ma', None, 'gy', 'gx'), may hold values from -6 to 6
- member_perts: bfloat16 [80, 2, 512, 512], P('ma', None, 'gy', 'gx'), may hold values from -0.625 to 0.625
- band_widths: int32 [2], replicated, may hold values from 2 to 8
- lat_index: int32 [1024], P('gy'), may hold values from 0 to 510, as said below
- lat_weight: float32 [1024], P('gy'), may hold values from 0 to 1
- lon_index: int32 [1024], P('gx'), may hold values from 0 to 511, as said below
- lon_weight: float32 [1024], P('gx'), may hold values from 0 to 1
- innovation: float32 [2, 1024, 1024], P(None, 'gy', 'gx'), may hold values from -6 to 6
- obs_weight: float32 [2, 1024, 1024], P(None, 'gy', 'gx'), may hold values from 0.1 to 1
Outputs:
- increment: float32 [2, 1024, 1024], P(None, 'gy', 'gx')
- gradient: float32 [80, 2, 512, 512], P('ma', None, 'gy', 'gx')
Inputs may be any that keep to these rules, and one draw needn't show every extreme that they name: lat_index[p] is p // 2 - 1 or p // 2, clamped to 0 .. 510. lon_index[q] is q // 2 - 1 or q // 2, taken modulo 512.
All inputs are finite; a program needn't handle non-finite values.
Results may differ from a plain program's by a relative error of at most 0.0003.
Values may be sent and summed in bfloat16 or wider, within the bound.
A program may use at most 128 MiB of HBM per device.

v0:
```python
import jax
import jax.numpy as jnp
from jax import lax
from jax.sharding import PartitionSpec as P

HB = 8


def padded_2(block, sides, width, periodic):
    for axis, dim in sides:
        count = lax.axis_size(axis)
        forward = [(i, i + 1) for i in range(count - 1)]
        if periodic:
            forward.append((count - 1, 0))
        backward = [(target, source) for source, target in forward]
        low = lax.ppermute(
            lax.slice_in_dim(block, block.shape[dim] - width, None, axis=dim), axis, forward
        )
        high = lax.ppermute(lax.slice_in_dim(block, 0, width, axis=dim), axis, backward)
        block = jnp.concatenate([low, block, high], axis=dim)
    return block


def tap_table(band_widths):
    tap_offsets = jnp.arange(-HB, HB + 1).astype(jnp.float32)
    spread = band_widths.astype(jnp.float32)[:, None]
    shapes = jnp.exp(-tap_offsets[None, :] ** 2 / (2.0 * spread * spread))
    return shapes / jnp.sqrt(jnp.sum(shapes * shapes, axis=1, keepdims=True))


def band_matrix(filter_taps, length):
    row_index = jnp.arange(length + 2 * HB, dtype=jnp.int32)[None, :, None]
    col_index = jnp.arange(length, dtype=jnp.int32)[None, None, :]
    tap_index = jnp.arange(2 * HB + 1, dtype=jnp.int32)[:, None, None]
    onehot = (row_index - col_index == tap_index).astype(jnp.float32)
    return jnp.einsum("ld,dkj->lkj", filter_taps, onehot, precision=lax.Precision.HIGHEST)


def lon_filter(padded, lon_matrix):
    return jnp.einsum("mlik,lkj->mlij", padded, lon_matrix, precision=lax.Precision.HIGHEST)


def lat_local(padded, lat_matrix):
    return jnp.einsum("mlkj,lki->mlij", padded, lat_matrix, precision=lax.Precision.HIGHEST)


def lat_filter(source, lat_matrix):
    padded = padded_2(source, (("gy", 2),), HB, False)
    return lat_local(padded, lat_matrix)


def stencil(relative, weight, length):
    columns = jnp.arange(length, dtype=jnp.int32)[None, :]
    near_cell = (columns == relative[:, None]).astype(jnp.float32)
    next_cell = (columns == relative[:, None] + 1).astype(jnp.float32)
    return (1.0 - weight[:, None]) * near_cell + weight[:, None] * next_cell


def fine_step(coarse, target, weights, lat_map, lon_map):
    framed = padded_2(coarse, (("gx", 2), ("gy", 1)), 1, True)
    by_lat = jnp.einsum("pa,lab->lpb", lat_map, framed, precision=lax.Precision.HIGHEST)
    increment = jnp.einsum("lpb,qb->lpq", by_lat, lon_map, precision=lax.Precision.HIGHEST)
    misfit = weights * (increment - target)
    lon_back = jnp.einsum("lpq,qb->lpb", misfit, lon_map, precision=lax.Precision.HIGHEST)
    restricted = jnp.einsum("pa,lpb->lab", lat_map, lon_back, precision=lax.Precision.HIGHEST)
    lon_edges = jnp.stack((restricted[:, :, 0], restricted[:, :, -1]), axis=2)
    received = padded_2(lon_edges, (("gx", 2),), 1, True)
    folded = restricted[:, :, 1:-1]
    folded = folded.at[:, :, 0].add(received[:, :, 0]).at[:, :, -1].add(received[:, :, 3])
    lat_edges = jnp.stack((folded[:, 0, :], folded[:, -1, :]), axis=1)
    arrived = padded_2(lat_edges, (("gy", 1),), 1, False)
    residual = folded[:, 1:-1, :]
    residual = residual.at[:, 0, :].add(arrived[:, 0, :]).at[:, -1, :].add(arrived[:, 3, :])
    return (increment, residual)


def body(
    alpha_fields,
    member_perts,
    band_widths,
    lat_index,
    lat_weight,
    lon_index,
    lon_weight,
    innovation,
    obs_weight,
):
    shard_lat = alpha_fields.shape[2]
    shard_lon = alpha_fields.shape[3]
    filter_taps = tap_table(band_widths)
    lon_matrix = band_matrix(filter_taps, shard_lon)
    lat_matrix = band_matrix(filter_taps, shard_lat)
    alpha_wide = padded_2(alpha_fields, (("gx", 3),), HB, True)
    localized = lat_filter(lon_filter(alpha_wide.astype(jnp.float32), lon_matrix), lat_matrix)
    local_sum = jnp.sum(member_perts.astype(jnp.float32) * localized, axis=0)
    lat_start = lax.axis_index("gy") * shard_lat
    lon_start = lax.axis_index("gx") * shard_lon
    lon_total = shard_lon * lax.axis_size("gx")
    lat_map = stencil(lat_index - lat_start + 1, lat_weight, shard_lat + 2)
    lon_map = stencil(
        jnp.remainder(lon_index - lon_start + 1, lon_total), lon_weight, shard_lon + 2
    )
    level_share = lax.psum_scatter(local_sum, "ma", scatter_dimension=0, tiled=True)
    levels_here = level_share.shape[0]
    first_level = lax.axis_index("ma") * levels_here
    own_target = lax.dynamic_slice_in_dim(innovation, first_level, levels_here, 0)
    own_weight = lax.dynamic_slice_in_dim(obs_weight, first_level, levels_here, 0)
    part_increment, part_residual = fine_step(level_share, own_target, own_weight, lat_map, lon_map)
    increment = lax.all_gather(part_increment, "ma", axis=0, tiled=True)
    coarse_residual = lax.all_gather(part_residual, "ma", axis=0, tiled=True)
    products = padded_2(
        member_perts.astype(jnp.float32) * coarse_residual[None], (("gx", 3),), HB, True
    )
    gradient = alpha_fields.astype(jnp.float32) + lat_filter(
        lon_filter(products, lon_matrix), lat_matrix
    )
    return (increment, gradient)


def solution(mesh):
    placed = (
        P("ma", None, "gy", "gx"),
        P("ma", None, "gy", "gx"),
        P(),
        P("gy"),
        P("gy"),
        P("gx"),
        P("gx"),
        P(None, "gy", "gx"),
        P(None, "gy", "gx"),
    )
    return jax.shard_map(
        body,
        mesh=mesh,
        in_specs=placed,
        out_specs=(P(None, "gy", "gx"), P("ma", None, "gy", "gx")),
        check_vma=False,
    )
```

profile of v0, /device:TPU:0, one launch (start us, length us, event | category | flops | bytes accessed | tf_op | source)
XLA Modules:
  0.0 171.9 jit_solution(5458942289306915994)
XLA Ops:
  7.2 3.3 %copy.24 = bf16[40,2,128,128]{2,3,0,1:T(8,128)(2,1)S(1)} copy(bf16[40,2,128,128]{3,2,1,0:T(8,128)(2,1)} %param.17) | data formatting | bytes 5242880 | tf_op args[0]
  10.6 3.0 %collective-permute-start = (bf16[40,2,128,8]{2,3,0,1:T(8,128)(2,1)S(1)}, bf16[40,2,128,8]{2,3,0,1:T(8,128)(2,1)S(1)}, u32[]{:S(2)}, u32[]{:S(2)}) collective-permute-start(bf16[40,2,128,8]{2,3,0,1:T(8,128)(2,1)S(1)} %get-tuple-element.62), channel_id=1, source_target_pairs={{0,8},{8,16},{16,24},{24,0},{1,9},{9,17},{17,25},{25,1},{2,10},{10... | collective-permute-start | bytes 491528 | tf_op jit(solution)/shard_map/ppermute | solution.py:16
  15.5 4.1 %collective-permute-done = bf16[40,2,128,8]{2,3,0,1:T(8,128)(2,1)S(1)} collective-permute-done((bf16[40,2,128,8]{2,3,0,1:T(8,128)(2,1)S(1)}, bf16[40,2,128,8]{2,3,0,1:T(8,128)(2,1)S(1)}, u32[]{:S(2)}, u32[]{:S(2)}) %collective-permute-start) | collective-permute-done | bytes 163872 | tf_op jit(solution)/shard_map/ppermute | solution.py:16
  19.6 2.9 %collective-permute-done.1 = bf16[40,2,128,8]{2,3,0,1:T(8,128)(2,1)S(1)} collective-permute-done((bf16[40,2,128,8]{2,3,0,1:T(8,128)(2,1)S(1)}, bf16[40,2,128,8]{2,3,0,1:T(8,128)(2,1)S(1)}, u32[]{:S(2)}, u32[]{:S(2)}) %collective-permute-start.1) | collective-permute-done | bytes 163872 | tf_op jit(solution)/shard_map/ppermute | solution.py:19
  22.5 5.5 %fusion.25 = f32[40,2,128,128]{3,2,0,1:T(8,128)S(1)} fusion(bf16[40,2,128,8]{2,3,0,1:T(8,128)(2,1)S(1)} %collective-permute-done.1, bf16[40,2,128,128]{2,3,0,1:T(8,128)(2,1)S(1)} %copy.24, bf16[40,2,128,8]{2,3,0,1:T(8,128)(2,1)S(1)} %collective-permute-done, f32[2,144,128,1]{2,0,1,3:T(2,128)S(1)} %fusion.36), kind=kOutput, calls=%fused_computation.28 | convolution fusion | flops 2273771520 | bytes 8339456 | tf_op jit(solution)/shard_map/mlik,lkj->mlij/dot_general | solution.py:40
  28.0 2.3 %copy-done.2 = f32[40,2,128,128]{3,2,0,1:T(8,128)} copy-done((f32[40,2,128,128]{3,2,0,1:T(8,128)}, f32[40,2,128,128]{3,2,0,1:T(8,128)S(1)}, u32[]{:S(2)}) %copy-start.2) | copy-done | bytes 5242904
  30.4 3.5 %collective-permute-start.2 = (f32[40,2,8,128]{3,2,0,1:T(8,128)S(1)}, f32[40,2,8,128]{3,2,0,1:T(8,128)S(1)}, u32[]{:S(2)}, u32[]{:S(2)}) collective-permute-start(f32[40,2,8,128]{3,2,0,1:T(8,128)S(1)} %get-tuple-element.60), channel_id=1, source_target_pairs={{0,2},{2,4},{4,6},{1,3},{3,5},{5,7},{8,10},{10,12},{12,14},{9,11},... | collective-permute-start | bytes 983048 | tf_op jit(solution)/shard_map/ppermute | solution.py:16
  35.4 4.5 %collective-permute-done.2 = f32[40,2,8,128]{3,2,0,1:T(8,128)S(1)} collective-permute-done((f32[40,2,8,128]{3,2,0,1:T(8,128)S(1)}, f32[40,2,8,128]{3,2,0,1:T(8,128)S(1)}, u32[]{:S(2)}, u32[]{:S(2)}) %collective-permute-start.2) | collective-permute-done | bytes 327712 | tf_op jit(solution)/shard_map/ppermute | solution.py:16
  40.0 4.1 %collective-permute-done.3 = f32[40,2,8,128]{3,2,0,1:T(8,128)S(1)} collective-permute-done((f32[40,2,8,128]{3,2,0,1:T(8,128)S(1)}, f32[40,2,8,128]{3,2,0,1:T(8,128)S(1)}, u32[]{:S(2)}, u32[]{:S(2)}) %collective-permute-start.3) | collective-permute-done | bytes 327712 | tf_op jit(solution)/shard_map/ppermute | solution.py:19
  44.1 9.6 %fusion.18 = f32[2,128,128]{2,1,0:T(8,128)} fusion(f32[40,2,8,128]{3,2,0,1:T(8,128)S(1)} %collective-permute-done.3, f32[40,2,128,128]{3,2,0,1:T(8,128)} %copy-done.2, f32[40,2,8,128]{3,2,0,1:T(8,128)S(1)} %collective-permute-done.2, bf16[40,2,128,128]{3,2,1,0:T(8,128)(2,1)} %param.18, f32[2,144,128,1]{2,0,1,3:T(2,128)S(1)} %fusion.36), kind=kOutput, calls=%fused_computation.20 | convolution fusion | flops 2271772672 | bytes 8798208 | tf_op jit(solution)/shard_map/mlkj,lki->mlij/dot_general | solution.py:44
  53.8 6.9 %reduce-scatter.2.cloned.1.call-done = f32[1,128,128]{2,1,0:T(8,128)} async-done(((f32[2,128,128]{2,1,0:T(8,128)}), f32[1,128,128]{2,1,0:T(8,128)}) %reduce-scatter.2.cloned.1.call-update) | async-done | bytes 65552 | tf_op jit(solution)/shard_map/reduce_scatter | solution.py:103
  61.7 1.7 %collective-permute-start.4 = (f32[1,128,1]{2,1,0:T(8,128)S(1)}, f32[1,128,1]{2,1,0:T(8,128)S(1)}, u32[]{:S(2)}, u32[]{:S(2)}) collective-permute-start(f32[1,128,1]{2,1,0:T(8,128)S(1)} %get-tuple-element.70), channel_id=1, source_target_pairs={{0,8},{8,16},{16,24},{24,0},{1,9},{9,17},{17,25},{25,1},{2,10},{10... | collective-permute-start | bytes 1544 | tf_op jit(solution)/shard_map/ppermute | solution.py:16
  64.7 2.3 %collective-permute-done.4 = f32[1,128,1]{2,1,0:T(8,128)S(1)} collective-permute-done((f32[1,128,1]{2,1,0:T(8,128)S(1)}, f32[1,128,1]{2,1,0:T(8,128)S(1)}, u32[]{:S(2)}, u32[]{:S(2)}) %collective-permute-start.4) | collective-permute-done | bytes 544 | tf_op jit(solution)/shard_map/ppermute | solution.py:16
  67.0 1.7 collective-permute-done.5
  70.9 2.3 %collective-permute-start.7 = (f32[1,1,130]{2,1,0:T(1,128)S(1)}, f32[1,1,130]{2,1,0:T(1,128)S(1)}, u32[]{:S(2)}, u32[]{:S(2)}) collective-permute-start(f32[1,1,130]{2,1,0:T(1,128)S(1)} %get-tuple-element.65), channel_id=1, source_target_pairs={{2,0},{4,2},{6,4},{0,6},{3,1},{5,3},{7,5},{1,7},{10,8},{12,10},{14... | collective-permute-start | bytes 1568 | tf_op jit(solution)/shard_map/ppermute | solution.py:19
  84.7 3.1 %collective-permute-start.10 = (f32[1,1,128]{1,2,0:T(8,128)S(1)}, f32[1,1,128]{1,2,0:T(8,128)S(1)}, u32[]{:S(2)}, u32[]{:S(2)}) collective-permute-start(f32[1,1,128]{1,2,0:T(8,128)S(1)} %get-tuple-element.69), channel_id=1, source_target_pairs={{0,2},{2,4},{4,6},{1,3},{3,5},{5,7},{8,10},{10,12},{12,14},{9,11},... | collective-permute-start | bytes 1544 | tf_op jit(solution)/shard_map/ppermute | solution.py:16
  90.1 4.0 %collective-permute-done.11 = f32[1,1,128]{1,2,0:T(8,128)S(1)} collective-permute-done((f32[1,1,128]{1,2,0:T(8,128)S(1)}, f32[1,1,128]{1,2,0:T(8,128)S(1)}, u32[]{:S(2)}, u32[]{:S(2)}) %collective-permute-start.11) | collective-permute-done | bytes 544 | tf_op jit(solution)/shard_map/ppermute | solution.py:19
  94.6 2.1 %all_gather.7 = f32[2,128,128]{2,1,0:T(8,128)S(1)} all-gather(f32[1,128,128]{2,1,0:T(8,128)S(1)} %copy.30), channel_id=1, replica_groups=mesh['gx'=4,'gy'=4,'ma'=2] {'ma'}, dimensions={0}, use_global_device_ids=true | all-gather | bytes 196608 | tf_op jit(solution)/shard_map/all_gather | solution.py:110
  97.5 5.8 %fusion.92 = (f32[40,2,128,8]{3,2,0,1:T(8,128)}, f32[40,2,128,8]{3,2,0,1:T(8,128)}) fusion(f32[40,2,128,128]{3,2,0,1:T(8,128)S(1)} %convert_multiply_fusion), kind=kLoop, calls=%fused_computation.117 | loop fusion | bytes 1310720 | tf_op jit(solution)/shard_map/slice | solution.py:17
  103.3 3.2 %copy.31 = f32[40,2,128,8]{2,3,1,0:T(8,128)S(1)} copy(f32[40,2,128,8]{3,2,0,1:T(8,128)} %get-tuple-element.58) | data formatting | bytes 655360 | tf_op jit(solution)/shard_map/slice | solution.py:17
  108.1 3.2 %copy.32 = f32[40,2,128,8]{2,3,1,0:T(8,128)S(1)} copy(f32[40,2,128,8]{3,2,0,1:T(8,128)} %get-tuple-element.59) | data formatting | bytes 655360 | tf_op jit(solution)/shard_map/slice | solution.py:19
  112.8 5.3 %collective-permute-done.12 = f32[40,2,128,8]{2,3,1,0:T(8,128)S(1)} collective-permute-done((f32[40,2,128,8]{2,3,1,0:T(8,128)S(1)}, f32[40,2,128,8]{2,3,1,0:T(8,128)S(1)}, u32[]{:S(2)}, u32[]{:S(2)}) %collective-permute-start.12) | collective-permute-done | bytes 327712 | tf_op jit(solution)/shard_map/ppermute | solution.py:16
  118.0 3.1 %copy.33 = f32[40,2,128,8]{3,2,0,1:T(8,128)} copy(f32[40,2,128,8]{2,3,1,0:T(8,128)S(1)} %collective-permute-done.12) | data formatting | bytes 655360 | tf_op jit(solution)/shard_map/ppermute | solution.py:16
  121.2 2.1 %collective-permute-done.13 = f32[40,2,128,8]{2,3,1,0:T(8,128)S(1)} collective-permute-done((f32[40,2,128,8]{2,3,1,0:T(8,128)S(1)}, f32[40,2,128,8]{2,3,1,0:T(8,128)S(1)}, u32[]{:S(2)}, u32[]{:S(2)}) %collective-permute-start.13) | collective-permute-done | bytes 327712 | tf_op jit(solution)/shard_map/ppermute | solution.py:19
  123.3 3.1 %copy.34 = f32[40,2,128,8]{3,2,0,1:T(8,128)} copy(f32[40,2,128,8]{2,3,1,0:T(8,128)S(1)} %collective-permute-done.13) | data formatting | bytes 655360 | tf_op jit(solution)/shard_map/ppermute | solution.py:19
  126.5 14.3 %fusion.32 = f32[40,2,128,128]{3,2,0,1:T(8,128)S(1)} fusion(f32[40,2,128,8]{3,2,0,1:T(8,128)} %copy.34, f32[40,2,128,128]{3,2,0,1:T(8,128)} %copy-done, f32[40,2,128,8]{3,2,0,1:T(8,128)} %copy.33, f32[2,144,128,1]{2,0,1,3:T(2,128)S(1)} %fusion.36), kind=kOutput, calls=%fused_computation.29 | convolution fusion | flops 2267873280 | bytes 11288576 | tf_op jit(solution)/shard_map/mlik,lkj->mlij/dot_general | solution.py:40
  140.9 3.7 %collective-permute-start.14 = (f32[40,2,8,128]{3,2,0,1:T(8,128)S(1)}, f32[40,2,8,128]{3,2,0,1:T(8,128)S(1)}, u32[]{:S(2)}, u32[]{:S(2)}) collective-permute-start(f32[40,2,8,128]{3,2,0,1:T(8,128)S(1)} %get-tuple-element.56), channel_id=1, source_target_pairs={{0,2},{2,4},{4,6},{1,3},{3,5},{5,7},{8,10},{10,12},{12,14},{9,11},... | collective-permute-start | bytes 983048 | tf_op jit(solution)/shard_map/ppermute | solution.py:16
  145.9 2.4 %all-gather = f32[512,256]{1,0:T(8,128)S(1)} all-gather(f32[256,256]{1,0:T(8,128)S(1)} %fusion.44), channel_id=2, replica_groups=mesh['gx'=4,'gy'=4,'ma'=2] {'ma'}, dimensions={0}, use_global_device_ids=true | all-gather | bytes 786432 | tf_op jit(solution)/shard_map/all_gather | solution.py:109
  148.3 2.7 %collective-permute-done.14 = f32[40,2,8,128]{3,2,0,1:T(8,128)S(1)} collective-permute-done((f32[40,2,8,128]{3,2,0,1:T(8,128)S(1)}, f32[40,2,8,128]{3,2,0,1:T(8,128)S(1)}, u32[]{:S(2)}, u32[]{:S(2)}) %collective-permute-start.14) | collective-permute-done | bytes 327712 | tf_op jit(solution)/shard_map/ppermute | solution.py:16
  151.0 4.4 %collective-permute-done.15 = f32[40,2,8,128]{3,2,0,1:T(8,128)S(1)} collective-permute-done((f32[40,2,8,128]{3,2,0,1:T(8,128)S(1)}, f32[40,2,8,128]{3,2,0,1:T(8,128)S(1)}, u32[]{:S(2)}, u32[]{:S(2)}) %collective-permute-start.15) | collective-permute-done | bytes 327712 | tf_op jit(solution)/shard_map/ppermute | solution.py:19
  155.4 5.9 %bitcast_add_fusion = f32[40,2,128,128]{3,2,0,1:T(8,128)S(1)} fusion(bf16[40,2,128,128]{3,2,1,0:T(8,128)(2,1)S(1)} %copy-done.1, f32[40,2,8,128]{3,2,0,1:T(8,128)S(1)} %collective-permute-done.15, f32[40,2,128,128]{3,2,0,1:T(8,128)S(1)} %fusion.32, f32[40,2,8,128]{3,2,0,1:T(8,128)S(1)} %collective-permute-done.14, f32[2,144,128,1]{2,0,1,3:T(2,128)S(1)} %fusion.36), kind=kOutput, calls=%fused_computation.21 | convolution fusion | flops 2270494720 | bytes 13910016 | tf_op jit(solution)/shard_map/mlkj,lki->mlij/dot_general | solution.py:44
  161.3 3.0 %copy.38 = f32[40,2,128,128]{3,2,1,0:T(8,128)} copy(f32[40,2,128,128]{3,2,0,1:T(8,128)S(1)} %bitcast_add_fusion) | data formatting | bytes 10485760
  (68 shorter events, 28.2 us)
Async XLA Ops:
  7.2 7.5 %copy-start.8 = (s32[2]{0:T(128)S(1)}, s32[2]{0:T(128)}, u32[]{:S(2)}) copy-start(s32[2]{0:T(128)} %param.19) | copy-start | bytes 28
  7.2 53.5 %reduce-scatter.2.cloned.1.call-start = ((), (), s32[]{:S(2)}) async-start(), calls=%async_computation.1 | async-start | bytes 196608 | tf_op jit(solution)/shard_map/reduce_scatter | solution.py:103
  10.6 9.0 %collective-permute-start = (bf16[40,2,128,8]{2,3,0,1:T(8,128)(2,1)S(1)}, bf16[40,2,128,8]{2,3,0,1:T(8,128)(2,1)S(1)}, u32[]{:S(2)}, u32[]{:S(2)}) collective-permute-start(bf16[40,2,128,8]{2,3,0,1:T(8,128)(2,1)S(1)} %get-tuple-element.62), channel_id=1, source_target_pairs={{0,8},{8,16},{16,24},{24,0},{1,9},{9,17},{17,25},{25,1},{2,10},{10... | collective-permute-start | bytes 491528 | tf_op jit(solution)/shard_map/ppermute | solution.py:16
  13.6 8.9 %collective-permute-start.1 = (bf16[40,2,128,8]{2,3,0,1:T(8,128)(2,1)S(1)}, bf16[40,2,128,8]{2,3,0,1:T(8,128)(2,1)S(1)}, u32[]{:S(2)}, u32[]{:S(2)}) collective-permute-start(bf16[40,2,128,8]{2,3,0,1:T(8,128)(2,1)S(1)} %get-tuple-element.63), channel_id=1, source_target_pairs={{8,0},{16,8},{24,16},{0,24},{9,1},{17,9},{25,17},{1,25},{10,2},{18... | collective-permute-start | bytes 491528 | tf_op jit(solution)/shard_map/ppermute | solution.py:19
  28.0 2.4 %copy-start.2 = (f32[40,2,128,128]{3,2,0,1:T(8,128)}, f32[40,2,128,128]{3,2,0,1:T(8,128)S(1)}, u32[]{:S(2)}) copy-start(f32[40,2,128,128]{3,2,0,1:T(8,128)S(1)} %fusion.25) | copy-start | bytes 15728644
  30.4 9.6 %collective-permute-start.2 = (f32[40,2,8,128]{3,2,0,1:T(8,128)S(1)}, f32[40,2,8,128]{3,2,0,1:T(8,128)S(1)}, u32[]{:S(2)}, u32[]{:S(2)}) collective-permute-start(f32[40,2,8,128]{3,2,0,1:T(8,128)S(1)} %get-tuple-element.60), channel_id=1, source_target_pairs={{0,2},{2,4},{4,6},{1,3},{3,5},{5,7},{8,10},{10,12},{12,14},{9,11},... | collective-permute-start | bytes 983048 | tf_op jit(solution)/shard_map/ppermute | solution.py:16
  33.9 10.2 %collective-permute-start.3 = (f32[40,2,8,128]{3,2,0,1:T(8,128)S(1)}, f32[40,2,8,128]{3,2,0,1:T(8,128)S(1)}, u32[]{:S(2)}, u32[]{:S(2)}) collective-permute-start(f32[40,2,8,128]{3,2,0,1:T(8,128)S(1)} %get-tuple-element.61), channel_id=1, source_target_pairs={{2,0},{4,2},{6,4},{3,1},{5,3},{7,5},{10,8},{12,10},{14,12},{11,9},... | collective-permute-start | bytes 983048 | tf_op jit(solution)/shard_map/ppermute | solution.py:19
  35.4 18.3 %copy-start.5 = (s32[256]{0:T(256)S(1)}, s32[256]{0:T(256)}, u32[]{:S(2)}) copy-start(s32[256]{0:T(256)} %param.20) | copy-start | bytes 3076
  35.4 18.4 %copy-start.6 = (s32[256]{0:T(256)S(1)}, s32[256]{0:T(256)}, u32[]{:S(2)}) copy-start(s32[256]{0:T(256)} %param.22) | copy-start | bytes 3076
  35.4 29.3 %copy-start.7 = (f32[256]{0:T(256)S(1)}, f32[256]{0:T(256)}, u32[]{:S(2)}) copy-start(f32[256]{0:T(256)} %param.21) | copy-start | bytes 3076
  35.4 37.8 %copy-start.4 = (f32[256]{0:T(256)S(1)}, f32[256]{0:T(256)}, u32[]{:S(2)}) copy-start(f32[256]{0:T(256)} %param.23) | copy-start | bytes 3076
  53.7 43.0 %copy-start.3 = (bf16[40,2,128,128]{3,2,1,0:T(8,128)(2,1)S(1)}, bf16[40,2,128,128]{3,2,1,0:T(8,128)(2,1)}, u32[]{:S(2)}) copy-start(bf16[40,2,128,128]{3,2,1,0:T(8,128)(2,1)} %param.18) | copy-start | bytes 7864324
  61.7 5.3 %collective-permute-start.4 = (f32[1,128,1]{2,1,0:T(8,128)S(1)}, f32[1,128,1]{2,1,0:T(8,128)S(1)}, u32[]{:S(2)}, u32[]{:S(2)}) collective-permute-start(f32[1,128,1]{2,1,0:T(8,128)S(1)} %get-tuple-element.70), channel_id=1, source_target_pairs={{0,8},{8,16},{16,24},{24,0},{1,9},{9,17},{17,25},{25,1},{2,10},{10... | collective-permute-start | bytes 1544 | tf_op jit(solution)/shard_map/ppermute | solution.py:16
  63.5 5.2 %collective-permute-start.5 = (f32[1,128,1]{2,1,0:T(8,128)S(1)}, f32[1,128,1]{2,1,0:T(8,128)S(1)}, u32[]{:S(2)}, u32[]{:S(2)}) collective-permute-start(f32[1,128,1]{2,1,0:T(8,128)S(1)} %get-tuple-element.71), channel_id=1, source_target_pairs={{8,0},{16,8},{24,16},{0,24},{9,1},{17,9},{25,17},{1,25},{10,2},{18... | collective-permute-start | bytes 1544 | tf_op jit(solution)/shard_map/ppermute | solution.py:19
  69.4 5.4 %collective-permute-start.6 = (f32[1,1,130]{2,1,0:T(1,128)S(1)}, f32[1,1,130]{2,1,0:T(1,128)S(1)}, u32[]{:S(2)}, u32[]{:S(2)}) collective-permute-start(f32[1,1,130]{2,1,0:T(1,128)S(1)} %get-tuple-element.64), channel_id=1, source_target_pairs={{0,2},{2,4},{4,6},{6,0},{1,3},{3,5},{5,7},{7,1},{8,10},{10,12},{12... | collective-permute-start | bytes 1568 | tf_op jit(solution)/shard_map/ppermute | solution.py:16
  70.9 3.9 %collective-permute-start.7 = (f32[1,1,130]{2,1,0:T(1,128)S(1)}, f32[1,1,130]{2,1,0:T(1,128)S(1)}, u32[]{:S(2)}, u32[]{:S(2)}) collective-permute-start(f32[1,1,130]{2,1,0:T(1,128)S(1)} %get-tuple-element.65), channel_id=1, source_target_pairs={{2,0},{4,2},{6,4},{0,6},{3,1},{5,3},{7,5},{1,7},{10,8},{12,10},{14... | collective-permute-start | bytes 1568 | tf_op jit(solution)/shard_map/ppermute | solution.py:19
  79.5 4.5 %collective-permute-start.8 = (f32[1,130,1]{1,2,0:T(1,128)S(1)}, f32[1,130,1]{1,2,0:T(1,128)S(1)}, u32[]{:S(2)}, u32[]{:S(2)}) collective-permute-start(f32[1,130,1]{1,2,0:T(1,128)S(1)} %get-tuple-element.67), channel_id=1, source_target_pairs={{0,8},{8,16},{16,24},{24,0},{1,9},{9,17},{17,25},{25,1},{2,10},{10... | collective-permute-start | bytes 1568 | tf_op jit(solution)/shard_map/ppermute | solution.py:16
  81.0 3.6 %collective-permute-start.9 = (f32[1,130,1]{1,2,0:T(1,128)S(1)}, f32[1,130,1]{1,2,0:T(1,128)S(1)}, u32[]{:S(2)}, u32[]{:S(2)}) collective-permute-start(f32[1,130,1]{1,2,0:T(1,128)S(1)} %get-tuple-element.66), channel_id=1, source_target_pairs={{8,0},{16,8},{24,16},{0,24},{9,1},{17,9},{25,17},{1,25},{10,2},{18... | collective-permute-start | bytes 1568 | tf_op jit(solution)/shard_map/ppermute | solution.py:19
  84.7 5.0 %collective-permute-start.10 = (f32[1,1,128]{1,2,0:T(8,128)S(1)}, f32[1,1,128]{1,2,0:T(8,128)S(1)}, u32[]{:S(2)}, u32[]{:S(2)}) collective-permute-start(f32[1,1,128]{1,2,0:T(8,128)S(1)} %get-tuple-element.69), channel_id=1, source_target_pairs={{0,2},{2,4},{4,6},{1,3},{3,5},{5,7},{8,10},{10,12},{12,14},{9,11},... | collective-permute-start | bytes 1544 | tf_op jit(solution)/shard_map/ppermute | solution.py:16
  87.9 6.2 %collective-permute-start.11 = (f32[1,1,128]{1,2,0:T(8,128)S(1)}, f32[1,1,128]{1,2,0:T(8,128)S(1)}, u32[]{:S(2)}, u32[]{:S(2)}) collective-permute-start(f32[1,1,128]{1,2,0:T(8,128)S(1)} %get-tuple-element.68), channel_id=1, source_target_pairs={{2,0},{4,2},{6,4},{3,1},{5,3},{7,5},{10,8},{12,10},{14,12},{11,9},... | collective-permute-start | bytes 1544 | tf_op jit(solution)/shard_map/ppermute | solution.py:19
  97.4 5.8 %copy-start = (f32[40,2,128,128]{3,2,0,1:T(8,128)}, f32[40,2,128,128]{3,2,0,1:T(8,128)S(1)}, u32[]{:S(2)}) copy-start(f32[40,2,128,128]{3,2,0,1:T(8,128)S(1)} %convert_multiply_fusion) | copy-start | bytes 15728644
  106.5 11.5 %collective-permute-start.12 = (f32[40,2,128,8]{2,3,1,0:T(8,128)S(1)}, f32[40,2,128,8]{2,3,1,0:T(8,128)S(1)}, u32[]{:S(2)}, u32[]{:S(2)}) collective-permute-start(f32[40,2,128,8]{2,3,1,0:T(8,128)S(1)} %copy.31), channel_id=1, source_target_pairs={{0,8},{8,16},{16,24},{24,0},{1,9},{9,17},{17,25},{25,1},{2,10},{10... | collective-permute-start | bytes 983048 | tf_op jit(solution)/shard_map/ppermute | solution.py:16
  111.3 12.0 %collective-permute-start.13 = (f32[40,2,128,8]{2,3,1,0:T(8,128)S(1)}, f32[40,2,128,8]{2,3,1,0:T(8,128)S(1)}, u32[]{:S(2)}, u32[]{:S(2)}) collective-permute-start(f32[40,2,128,8]{2,3,1,0:T(8,128)S(1)} %copy.32), channel_id=1, source_target_pairs={{8,0},{16,8},{24,16},{0,24},{9,1},{17,9},{25,17},{1,25},{10,2},{18... | collective-permute-start | bytes 983048 | tf_op jit(solution)/shard_map/ppermute | solution.py:19
  126.5 28.9 %copy-start.1 = (bf16[40,2,128,128]{3,2,1,0:T(8,128)(2,1)S(1)}, bf16[40,2,128,128]{3,2,1,0:T(8,128)(2,1)}, u32[]{:S(2)}) copy-start(bf16[40,2,128,128]{3,2,1,0:T(8,128)(2,1)} %param.17) | copy-start | bytes 7864324
  140.9 10.1 %collective-permute-start.14 = (f32[40,2,8,128]{3,2,0,1:T(8,128)S(1)}, f32[40,2,8,128]{3,2,0,1:T(8,128)S(1)}, u32[]{:S(2)}, u32[]{:S(2)}) collective-permute-start(f32[40,2,8,128]{3,2,0,1:T(8,128)S(1)} %get-tuple-element.56), channel_id=1, source_target_pairs={{0,2},{2,4},{4,6},{1,3},{3,5},{5,7},{8,10},{10,12},{12,14},{9,11},... | collective-permute-start | bytes 983048 | tf_op jit(solution)/shard_map/ppermute | solution.py:16
  144.6 10.8 %collective-permute-start.15 = (f32[40,2,8,128]{3,2,0,1:T(8,128)S(1)}, f32[40,2,8,128]{3,2,0,1:T(8,128)S(1)}, u32[]{:S(2)}, u32[]{:S(2)}) collective-permute-start(f32[40,2,8,128]{3,2,0,1:T(8,128)S(1)} %get-tuple-element.57), channel_id=1, source_target_pairs={{2,0},{4,2},{6,4},{3,1},{5,3},{7,5},{10,8},{12,10},{14,12},{11,9},... | collective-permute-start | bytes 983048 | tf_op jit(solution)/shard_map/ppermute | solution.py:19
Sparse Core Ops, SparseCore 0:
  53.8 6.8 reduce-scatter.1
where the time goes:
time: 172 us
  waiting for transfers between devices  49.1 us (29%)
  matrix products  40.7 us (24%)
  starting transfers between devices  31.2 us (18%)
  local copies, waits for them, and re-layouts  30.1 us (18%)
  between operations  14.4 us (8%)
  blocking collectives  4.56 us (3%)
  other arithmetic  1.89 us (1%)
    ppermute x8, waiting for transfers between devices, padded_2(): lax.ppermute(lax.slice_in_dim(block, block.shape[dim] - width, None, axis...  22.3 us
    ppermute x8, waiting for transfers between devices, padded_2(): lax.ppermute(lax.slice_in_dim(block, 0, width, axis=dim), axis, backward)  19.8 us
    dot_general x2, matrix products, lon_filter(): jnp.einsum('mlik,lkj->mlij', padded, lon_matrix, precision=lax.Precision....  19.8 us
    ppermute x8, starting transfers between devices, padded_2(): lax.ppermute(lax.slice_in_dim(block, block.shape[dim] - width, None, axis...  19.6 us
    dot_general x2, matrix products, lat_local(): jnp.einsum('mlkj,lki->mlij', padded, lat_matrix, precision=lax.Precision....  15.5 us
    ppermute x8, starting transfers between devices, padded_2(): lax.ppermute(lax.slice_in_dim(block, 0, width, axis=dim), axis, backward)  11.6 us
    slice x6, local copies, waits for them, and re-layouts, padded_2(): lax.slice_in_dim(block, block.shape[dim] - width, None, axis=dim)  10.2 us
    unnamed x21, local copies, waits for them, and re-layouts  9.41 us
  transfers between devices with their start and end apart: 17, of which 16 were waited for; matrix products, arithmetic and copies ran while one was open for 5% of the time, Pallas kernels for 0%

commit v1 on v0

v1 whole, which is shorter than its diff:
```python
import jax
import jax.numpy as jnp
from jax import lax
from jax.experimental import pallas as pl
from jax.experimental.pallas import tpu as pltpu
from jax.sharding import PartitionSpec as P

HB = 8
GROUP = 8
CH = HB + 2
FH = 2 * HB + 2
HIGHEST = lax.Precision.HIGHEST
F32 = jnp.float32
BF16 = jnp.bfloat16


def shifts(axis, periodic):
    count = lax.axis_size(axis)
    forward = [(i, i + 1) for i in range(count - 1)]
    if periodic:
        forward.append((count - 1, 0))
    return forward, [(target, source) for source, target in forward]


def swap_edges(low_edge, high_edge, axis, periodic):
    forward, backward = shifts(axis, periodic)
    return (
        lax.ppermute(high_edge, axis, forward),
        lax.ppermute(low_edge, axis, backward),
    )


def framed(block, axis, dim, width, periodic):
    size = block.shape[dim]
    low, high = swap_edges(
        lax.slice_in_dim(block, 0, width, axis=dim),
        lax.slice_in_dim(block, size - width, size, axis=dim),
        axis,
        periodic,
    )
    return jnp.concatenate([block, low, high], axis=dim)


def place(order, size, width):
    return jnp.where(order < size, order, jnp.where(order < size + width, order - size - width, order - width))


def tap_value(distance, spread, scale):
    d = distance.astype(F32)
    return jnp.where(jnp.abs(distance) <= HB, jnp.exp(-(d * d) / (2.0 * spread * spread)) * scale, 0.0)


def split_cols(value, column, half):
    high = lax.reduce_precision(value, 8, 7)
    return jnp.where(column < half, high, value - high).astype(BF16)


def filter_matrices(band_widths, rows, cols):
    levels = band_widths.shape[0]
    spread = band_widths.astype(F32)
    offsets = jnp.arange(-HB, HB + 1).astype(F32)
    shapes = jnp.exp(-(offsets[None, :] ** 2) / (2.0 * spread[:, None] * spread[:, None]))
    scale = 1.0 / jnp.sqrt(jnp.sum(shapes * shapes, axis=1))
    half = GROUP * HB
    shape = (levels, GROUP, cols + 2 * half, 2 * cols)
    l = lax.broadcasted_iota(jnp.int32, shape, 0)
    k = lax.broadcasted_iota(jnp.int32, shape, 1)
    r = lax.broadcasted_iota(jnp.int32, shape, 2)
    c = lax.broadcasted_iota(jnp.int32, shape, 3)
    q = r - cols
    west = (q // half) == l
    pos = jnp.where(r < cols, r, jnp.where(west, q % HB - HB, cols + q % HB))
    valid = (r < cols) | ((q % half) // HB == k)
    dist = jnp.where(valid, pos - c % cols, 2 * HB)
    lon = split_cols(tap_value(dist, spread[:, None, None, None], scale[:, None, None, None]), c, cols)
    shape = (levels, 2 * rows, rows + 2 * HB)
    i = lax.broadcasted_iota(jnp.int32, shape, 1)
    r = lax.broadcasted_iota(jnp.int32, shape, 2)
    dist = place(r, rows, HB) - i % rows
    lat = split_cols(tap_value(dist, spread[:, None, None], scale[:, None, None]), i, rows)
    return lon, lat


def dot(a, b):
    return jnp.dot(a, b, preferred_element_type=F32)


def rows16(north, south):
    return jnp.concatenate([north.astype(F32), south.astype(F32)], axis=0)


def pack_kernel(core, north, south, right, left, pick):
    cols = core.shape[3]
    half = GROUP * HB
    levels = core.shape[1]

    @pl.when(pl.program_id(0) == 0)
    def _():
        r = lax.broadcasted_iota(jnp.int32, (cols, 4 * half), 0)
        c = lax.broadcasted_iota(jnp.int32, (cols, 4 * half), 1)
        for l in range(levels):
            for k in range(GROUP):
                to_right = c - (l * half + HB * k)
                to_left = c - 2 * half - ((1 - l) * half + HB * k)
                hit = ((to_right >= 0) & (to_right < HB) & (r == cols - HB + to_right)) | (
                    (to_left >= 0) & (to_left < HB) & (r == to_left)
                )
                pick[l * GROUP + k] = jnp.where(hit, 1.0, 0.0).astype(BF16)

    total = None
    for l in range(levels):
        for k in range(GROUP):
            edge = rows16(north[k, l], south[k, l]).astype(BF16)
            part = dot(jnp.concatenate([core[k, l], edge], axis=0), pick[l * GROUP + k])
            total = part if total is None else total + part
    right[0] = total[:, : 2 * half].astype(BF16)
    left[0] = total[:, 2 * half :].astype(BF16)


def cost(flops, nbytes):
    return pl.CostEstimate(flops=flops, bytes_accessed=nbytes, transcendentals=0)


def pack(field, north, south):
    members, levels, rows, cols = field.shape
    steps = members // GROUP
    tall = rows + 2 * HB
    wide = 2 * GROUP * HB
    strip = pl.BlockSpec((GROUP, levels, HB, cols), lambda g: (g, 0, 0, 0))
    out = pl.BlockSpec((1, tall, wide), lambda g: (g, 0, 0))
    return pl.pallas_call(
        pack_kernel,
        grid=(steps,),
        in_specs=[pl.BlockSpec((GROUP, levels, rows, cols), lambda g: (g, 0, 0, 0)), strip, strip],
        out_specs=[out, out],
        out_shape=[jax.ShapeDtypeStruct((steps, tall, wide), BF16)] * 2,
        scratch_shapes=[pltpu.VMEM((levels * GROUP, cols, 2 * wide), BF16)],
        cost_estimate=cost(members * levels * tall * cols * wide * 4, field.size * 2),
    )(field, north, south)


def merged(west, east, level):
    lane = lax.broadcasted_iota(jnp.int32, west.shape, 1)
    w, e = west.astype(F32), east.astype(F32)
    a, b = (w, e) if level == 0 else (e, w)
    return jnp.where(lane < GROUP * HB, a, b)


def split(value):
    high = value.astype(BF16)
    return high, (value - high.astype(F32)).astype(BF16)


def lat_stage(u, lat_l):
    rows = lat_l.shape[0] // 2
    high, low = split(u)
    both = dot(lat_l, high)
    return both[:rows] + both[rows:] + dot(lat_l[:rows], low)


def forward_kernel(alpha, north, south, west, east, perts, lon, lat, out):
    cols = alpha.shape[3]

    @pl.when(pl.program_id(0) == 0)
    def _():
        out[...] = jnp.zeros_like(out)

    for l in range(alpha.shape[1]):
        side = merged(west[0], east[0], l).astype(BF16)
        total = None
        for k in range(GROUP):
            edge = rows16(north[k, l], south[k, l]).astype(BF16)
            tall = jnp.concatenate([alpha[k, l], edge], axis=0)
            both = dot(jnp.concatenate([tall, side], axis=1), lon[l, k])
            v = lat_stage(both[:, :cols] + both[:, cols:], lat[l])
            part = perts[k, l].astype(F32) * v
            total = part if total is None else total + part
        out[l] += total


def adjoint_kernel(alpha, perts, north, south, west, east, residual, lon, lat, out):
    cols = alpha.shape[3]
    rows = alpha.shape[2]
    for l in range(alpha.shape[1]):
        res = residual[l, :, :cols]
        side_h, side_l = split(merged(west[0], east[0], l) * residual[l, :, cols:])
        for k in range(GROUP):
            prod = jnp.concatenate(
                [
                    perts[k, l].astype(F32) * res[:rows],
                    rows16(north[k, l], south[k, l]) * res[rows:],
                ],
                axis=0,
            )
            high, low = split(prod)
            both = dot(jnp.concatenate([high, side_h], axis=1), lon[l, k])
            u = both[:, :cols] + both[:, cols:]
            u = u + dot(jnp.concatenate([low, side_l], axis=1), lon[l, k, :, :cols])
            out[k, l] = alpha[k, l].astype(F32) + lat_stage(u, lat[l])


def specs(alpha, lon, lat):
    members, levels, rows, cols = alpha.shape
    block = pl.BlockSpec((GROUP, levels, rows, cols), lambda g: (g, 0, 0, 0))
    strip = pl.BlockSpec((GROUP, levels, HB, cols), lambda g: (g, 0, 0, 0))
    side = pl.BlockSpec((1, rows + 2 * HB, 2 * GROUP * HB), lambda g: (g, 0, 0))
    lon_spec = pl.BlockSpec(lon.shape, lambda g: (0, 0, 0, 0))
    lat_spec = pl.BlockSpec(lat.shape, lambda g: (0, 0, 0))
    return block, strip, side, lon_spec, lat_spec


def forward(alpha, north, south, west, east, perts, lon, lat):
    members, levels, rows, cols = alpha.shape
    block, strip, side, lon_spec, lat_spec = specs(alpha, lon, lat)
    return pl.pallas_call(
        forward_kernel,
        grid=(members // GROUP,),
        in_specs=[block, strip, strip, side, side, block, lon_spec, lat_spec],
        out_specs=pl.BlockSpec((levels, rows, cols), lambda g: (0, 0, 0)),
        out_shape=jax.ShapeDtypeStruct((levels, rows, cols), F32),
        cost_estimate=cost(members * levels * 2**25, alpha.size * 4),
    )(alpha, north, south, west, east, perts, lon, lat)


def adjoint(alpha, perts, north, south, west, east, residual, lon, lat):
    members, levels, rows, cols = alpha.shape
    block, strip, side, lon_spec, lat_spec = specs(alpha, lon, lat)
    return pl.pallas_call(
        adjoint_kernel,
        grid=(members // GROUP,),
        in_specs=[
            block,
            block,
            strip,
            strip,
            side,
            side,
            pl.BlockSpec(residual.shape, lambda g: (0, 0, 0)),
            lon_spec,
            lat_spec,
        ],
        out_specs=block,
        out_shape=jax.ShapeDtypeStruct(alpha.shape, F32),
        cost_estimate=cost(members * levels * 2**25, alpha.size * 8),
    )(alpha, perts, north, south, west, east, residual, lon, lat)


def exact_dot(a, b):
    return jnp.dot(a, b, preferred_element_type=F32, precision=HIGHEST)


def weigh(cell, index, weight):
    return jnp.where(cell == index, 1.0 - weight, 0.0) + jnp.where(cell == index + 1, weight, 0.0)


def fine_kernel(coarse, fine, lat_col, lat_row, lon_col, lon_row, increment, residual):
    levels, rows, cols = coarse.shape[0], coarse.shape[1] - 2 * CH, coarse.shape[2] - 2 * CH
    tall, wide = fine.shape[2], fine.shape[3]
    half = GROUP * HB

    def iota(shape, dim):
        return lax.broadcasted_iota(jnp.int32, shape, dim)

    def col(ref):
        return ref[:, 0:1].astype(jnp.int32), ref[:, 1:2]

    def row(ref):
        return ref[0:1, :].astype(jnp.int32), ref[1:2, :]

    up_lat = weigh(place(iota((tall, rows + 2 * CH), 1), rows, CH), *col(lat_col))
    up_lon = weigh(place(iota((cols + 2 * CH, wide), 0), cols, CH), *row(lon_row))
    down_lat = weigh(place(iota((rows + 2 * HB, tall), 0), rows, HB), *row(lat_row))
    order = iota((wide, cols + 2 * half), 1)
    q = order - cols
    for l in range(levels):
        inc = exact_dot(exact_dot(up_lat, coarse[l]), up_lon)
        increment[l] = inc[: increment.shape[1], : increment.shape[2]]
        misfit = fine[1, l] * (inc - fine[0, l])
        west = (q // half) == l
        pos = jnp.where(order < cols, order, jnp.where(west, q % HB - HB, cols + q % HB))
        down_lon = weigh(pos, *col(lon_col))
        residual[l] = exact_dot(down_lat, exact_dot(misfit, down_lon))


def fine_step(coarse, fine, lat_data, lon_data, rows, cols, fine_rows, fine_cols):
    levels = coarse.shape[0]
    return pl.pallas_call(
        fine_kernel,
        out_shape=[
            jax.ShapeDtypeStruct((levels, fine_rows, fine_cols), F32),
            jax.ShapeDtypeStruct((levels, rows + 2 * HB, cols + 2 * GROUP * HB), F32),
        ],
        cost_estimate=cost(2**29, 2**21),
    )(coarse, fine, lat_data.T, lat_data, lon_data.T, lon_data)


def halo_fields(field):
    rows = field.shape[2]
    north, south = swap_edges(field[:, :, :HB], field[:, :, rows - HB :], "gy", False)
    right, left = pack(field, north, south)
    west, east = swap_edges(left, right, "gx", True)
    return north, south, west, east


def body(
    alpha_fields,
    member_perts,
    band_widths,
    lat_index,
    lat_weight,
    lon_index,
    lon_weight,
    innovation,
    obs_weight,
):
    rows, cols = alpha_fields.shape[2:]
    lon, lat = filter_matrices(band_widths, rows, cols)
    a_north, a_south, a_west, a_east = halo_fields(alpha_fields)
    p_north, p_south, p_west, p_east = halo_fields(member_perts)

    fine = jnp.stack([innovation, obs_weight])
    fine = framed(framed(fine, "gy", 2, FH, False), "gx", 3, FH, True)
    lat_start = lax.axis_index("gy") * rows
    lon_start = lax.axis_index("gx") * cols
    lon_total = cols * lax.axis_size("gx")
    lat_data = framed(jnp.stack([lat_index.astype(F32), lat_weight]), "gy", 1, FH, False)
    lon_data = framed(jnp.stack([lon_index.astype(F32), lon_weight]), "gx", 1, FH, True)
    lat_rel = lat_data[0] - lat_start.astype(F32)
    lon_rel = (
        jnp.remainder(lon_data[0].astype(jnp.int32) - lon_start + CH, lon_total) - CH
    ).astype(F32)
    lat_data = jnp.stack([lat_rel, lat_data[1]])
    lon_data = jnp.stack([lon_rel, lon_data[1]])

    partial = forward(alpha_fields, a_north, a_south, a_west, a_east, member_perts, lon, lat)
    count = lax.axis_size("ma")
    total = partial
    moving = partial
    for _ in range(count - 1):
        moving = lax.ppermute(moving, "ma", [(i, (i + 1) % count) for i in range(count)])
        total = total + moving
    coarse = framed(framed(total, "gx", 2, CH, True), "gy", 1, CH, False)
    increment, residual = fine_step(
        coarse, fine, lat_data, lon_data, rows, cols, innovation.shape[1], innovation.shape[2]
    )
    gradient = adjoint(
        alpha_fields, member_perts, p_north, p_south, p_west, p_east, residual, lon, lat
    )
    return (increment, gradient)


def solution(mesh):
    placed = (
        P("ma", None, "gy", "gx"),
        P("ma", None, "gy", "gx"),
        P(),
        P("gy"),
        P("gy"),
        P("gx"),
        P("gx"),
        P(None, "gy", "gx"),
        P(None, "gy", "gx"),
    )
    return jax.shard_map(
        body,
        mesh=mesh,
        in_specs=placed,
        out_specs=(P(None, "gy", "gx"), P("ma", None, "gy", "gx")),
        check_vma=False,
    )
```

time: 172 us -> 134 us (0.78)
  Pallas kernels: 0 us -> 56.9 us
  waiting for transfers between devices: 49.1 us -> 7.96 us
  matrix products: 40.7 us -> 0 us
  local copies, waits for them, and re-layouts: 30.1 us -> 8.65 us
  between operations: 14.4 us -> 1.04 us
  starting transfers between devices: 31.2 us -> 44.2 us
  other arithmetic: 1.89 us -> 14.7 us
  blocking collectives: 4.56 us -> 0 us
    pallas_call x0 -> x5, Pallas kernels: none -> 56.9 us  [the longest x1 23.7 us: adjoint(): pl.pallas_call(adjoint_kernel, grid=(members // GROUP,), in_specs=[block,...]
    dot_general x9 -> x0, matrix products: 40.7 us -> none  [the longest x2 19.8 us: lon_filter(): jnp.einsum('mlik,lkj->mlij', padded, lon_matrix, precision=lax.Precision....]
    ppermute x16 -> x21, waiting for transfers between devices: 42.2 us -> 7.96 us  [the longest x10 4.56 us: swap_edges(): lax.ppermute(high_edge, axis, forward)]
    ppermute x16 -> x21, starting transfers between devices: 31.2 us -> 44.2 us  [the longest x10 27.2 us: swap_edges(): lax.ppermute(high_edge, axis, forward)]
    slice x11 -> x7, local copies, waits for them, and re-layouts: 13.6 us -> 3.66 us  [the longest x2 2.81 us: halo_fields(): field[:, :, :HB]]
    convert_element_type x0 -> x5, other arithmetic: none -> 7.12 us  [the longest x2 5.65 us: split_cols(): return jnp.where(column < half, high, value - high).astype(BF16)]
    reduce_scatter x1 -> x0, waiting for transfers between devices: 6.93 us -> none  [body(): lax.psum_scatter(local_sum, 'ma', scatter_dimension=0, tiled=True)]
    unnamed x21 -> x28, local copies, waits for them, and re-layouts: 9.41 us -> 2.87 us
  transfers between devices with their start and end apart: 17 -> 21, of which waited for: 16 -> 3; matrix products, arithmetic and copies ran while one was open for 5% -> 14% of each run, Pallas kernels for 0% -> 25%
where the time goes in v1:
time: 134 us; the launch traced here: 133 us
  Pallas kernels  56.9 us (42%)
  starting transfers between devices  44.2 us (33%)
  other arithmetic  14.7 us (11%)
  local copies, waits for them, and re-layouts  8.65 us (6%)
  waiting for transfers between devices  7.96 us (6%)
    ppermute x10, starting transfers between devices, swap_edges(): lax.ppermute(high_edge, axis, forward)  27.2 us
    pallas_call x1, Pallas kernels, adjoint(): pl.pallas_call(adjoint_kernel, grid=(members // GROUP,), in_specs=[block,...  23.7 us
    ppermute x10, starting transfers between devices, swap_edges(): lax.ppermute(low_edge, axis, backward)  16.9 us
    pallas_call x1, Pallas kernels, forward(): pl.pallas_call(forward_kernel, grid=(members // GROUP,), in_specs=[block,...  14.4 us
    pallas_call x2, Pallas kernels, pack(): pl.pallas_call(pack_kernel, grid=(steps,), in_specs=[pl.BlockSpec((GROUP,...  11 us
    pallas_call x1, Pallas kernels, fine_step(): pl.pallas_call(fine_kernel, out_shape=[jax.ShapeDtypeStruct((levels, fine...  7.79 us
    convert_element_type x2, other arithmetic, split_cols(): return jnp.where(column < half, high, value - high).astype(BF16)  5.65 us
    ppermute x10, waiting for transfers between devices, swap_edges(): lax.ppermute(high_edge, axis, forward)  4.56 us
  transfers between devices with their start and end apart: 21, of which 3 were waited for; matrix products, arithmetic and copies ran while one was open for 14% of the time, Pallas kernels for 25%

profile of v1, /device:TPU:0, one launch (start us, length us, event | category | flops | bytes accessed | tf_op | source)
XLA Modules:
  0.0 133.4 jit_solution(7240701340392828119)
XLA Ops:
  2.2 4.9 %collective-permute-start.13 = (f32[2,18]{1,0:T(2,128)S(1)}, f32[2,18]{1,0:T(2,128)S(1)}, u32[]{:S(2)}, u32[]{:S(2)}) collective-permute-start(f32[2,18]{1,0:T(2,128)S(1)} %get-tuple-element.34), channel_id=1, source_target_pairs={{0,2},{2,4},{4,6},{1,3},{3,5},{5,7},{8,10},{10,12},{12,14},{9,11},... | collective-permute-start | bytes 440 | tf_op jit(solution)/shard_map/ppermute | solution.py:28
  7.1 1.3 collective-permute-start.14
  9.9 1.5 %collective-permute-start.15 = (f32[2,18]{1,0:T(2,128)S(1)}, f32[2,18]{1,0:T(2,128)S(1)}, u32[]{:S(2)}, u32[]{:S(2)}) collective-permute-start(f32[2,18]{1,0:T(2,128)S(1)} %get-tuple-element.32), channel_id=1, source_target_pairs={{0,8},{8,16},{16,24},{24,0},{1,9},{9,17},{17,25},{25,1},{2,10},{10... | collective-permute-start | bytes 440 | tf_op jit(solution)/shard_map/ppermute | solution.py:28
  11.4 1.4 %collective-permute-start.16 = (f32[2,18]{1,0:T(2,128)S(1)}, f32[2,18]{1,0:T(2,128)S(1)}, u32[]{:S(2)}, u32[]{:S(2)}) collective-permute-start(f32[2,18]{1,0:T(2,128)S(1)} %get-tuple-element.33), channel_id=1, source_target_pairs={{8,0},{16,8},{24,16},{0,24},{9,1},{17,9},{25,17},{1,25},{10,2},{18... | collective-permute-start | bytes 440 | tf_op jit(solution)/shard_map/ppermute | solution.py:29
  12.8 0.9 pad_maximum_fusion.4
  13.7 4.6 %collective-permute-start.9 = (f32[2,2,18,256]{3,2,1,0:T(8,128)S(1)}, f32[2,2,18,256]{3,2,1,0:T(8,128)S(1)}, u32[]{:S(2)}, u32[]{:S(2)}) collective-permute-start(f32[2,2,18,256]{3,2,1,0:T(8,128)S(1)} %get-tuple-element.20), channel_id=1, source_target_pairs={{0,2},{2,4},{4,6},{1,3},{3,5},{5,7},{8,10},{10,12},{12,14},{9,11},... | collective-permute-start | bytes 221192 | tf_op jit(solution)/shard_map/ppermute | solution.py:28
  19.3 1.0 fusion.27
  20.3 1.8 %fusion.26 = (bf16[40,2,8,128]{3,2,1,0:T(8,128)(2,1)}, bf16[40,2,8,128]{3,2,1,0:T(8,128)(2,1)}) fusion(bf16[40,2,128,128]{3,2,1,0:T(8,128)(2,1)} %perts.3), kind=kLoop, calls=%fused_computation.85 | loop fusion | bytes 655360 | tf_op jit(solution)/shard_map/slice | solution.py:299
  22.1 1.1 fusion.12.lat
  23.2 4.5 %fusion.6.lon = bf16[2,8,256,256]{3,2,1,0:T(8,128)(2,1)} fusion(f32[2]{0:T(128)S(1)} %sqrt.3, f32[2]{0:T(128)S(1)} %multiply_multiply_fusion, s32[256]{0:T(256)S(1)} %get-tuple-element.43, s32[256]{0:T(256)S(1)} %get-tuple-element.44, s32[256]{0:T(256)S(1)} %get-tuple-element.40, s32[256]{0:T(256)S(1)} %get-tuple-element.45, s32[256]{0:T(256)S(1)} %get-tuple-element.41, ...), kind=kLoop, calls=%fused_computation.16 | loop fusion | flops 41943040 | bytes 2106640 | tf_op jit(solution)/shard_map/convert_element_type | solution.py:55
  27.7 1.3 collective-permute-start.1
  29.0 4.6 %collective-permute-start = (bf16[40,2,8,128]{3,2,1,0:T(8,128)(2,1)S(1)}, bf16[40,2,8,128]{3,2,1,0:T(8,128)(2,1)S(1)}, u32[]{:S(2)}, u32[]{:S(2)}) collective-permute-start(bf16[40,2,8,128]{3,2,1,0:T(8,128)(2,1)S(1)} %get-tuple-element.17), channel_id=1, source_target_pairs={{0,2},{2,4},{4,6},{1,3},{3,5},{5,7},{8,10},{10,12},{12,14},{9,11},... | collective-permute-start | bytes 491528 | tf_op jit(solution)/shard_map/ppermute | solution.py:28
  33.7 1.3 collective-permute-start.10
  35.0 1.3 collective-permute-start.18
  37.7 5.5 %shard_map.104 = (bf16[5,144,128]{2,1,0:T(8,128)(2,1)}, bf16[5,144,128]{2,1,0:T(8,128)(2,1)}) custom-call(bf16[40,2,128,128]{3,2,1,0:T(8,128)(2,1)} %alpha.3, bf16[40,2,8,128]{3,2,1,0:T(8,128)(2,1)} %copy-done.9, bf16[40,2,8,128]{3,2,1,0:T(8,128)(2,1)} %copy-done.8), custom_call_target="tpu_custom_call" | custom-call | flops 754974720 | bytes 2621440 | tf_op jit(solution)/shard_map/pallas_call | solution.py:131
  43.8 2.3 %collective-permute-start.3 = (bf16[5,144,128]{2,1,0:T(8,128)(2,1)}, bf16[5,144,128]{2,1,0:T(8,128)(2,1)S(1)}, u32[]{:S(2)}, u32[]{:S(2)}) collective-permute-start(bf16[5,144,128]{2,1,0:T(8,128)(2,1)} %get-tuple-element.9), channel_id=1, source_target_pairs={{8,0},{16,8},{24,16},{0,24},{9,1},{17,9},{25,17},{1,25},{10,2},{18... | collective-permute-start | bytes 552968 | tf_op jit(solution)/shard_map/ppermute | solution.py:29
  46.2 5.9 %collective-permute-start.17 = (bf16[40,2,8,128]{3,2,1,0:T(8,128)(2,1)}, bf16[40,2,8,128]{3,2,1,0:T(8,128)(2,1)}, u32[]{:S(2)}, u32[]{:S(2)}) collective-permute-start(bf16[40,2,8,128]{3,2,1,0:T(8,128)(2,1)} %get-tuple-element.15), channel_id=1, source_target_pairs={{0,2},{2,4},{4,6},{1,3},{3,5},{5,7},{8,10},{10,12},{12,14},{9,11},... | collective-permute-start | bytes 491528 | tf_op jit(solution)/shard_map/ppermute | solution.py:28
  53.5 14.4 %shard_map.105 = f32[2,128,128]{2,1,0:T(8,128)} custom-call(bf16[40,2,128,128]{3,2,1,0:T(8,128)(2,1)} %alpha.3, bf16[40,2,8,128]{3,2,1,0:T(8,128)(2,1)} %copy-done.9, bf16[40,2,8,128]{3,2,1,0:T(8,128)(2,1)} %copy-done.8, bf16[5,144,128]{2,1,0:T(8,128)(2,1)} %copy-done.12, bf16[5,144,128]{2,1,0:T(8,128)(2,1)} %copy-done.13, bf16[40,2,128,128]{3,2,1,0:T(8,128)(2,1)} %perts.3, ...), custom_call_target="tpu_custom_call" | custom-call | flops 2684354560 | bytes 5242880 | tf_op jit(solution)/shard_map/pallas_call | solution.py:215
  69.5 1.4 %collective-permute-start.11 = (f32[2,2,292,18]{2,1,3,0:T(2,128)S(1)}, f32[2,2,292,18]{2,1,3,0:T(2,128)S(1)}, u32[]{:S(2)}, u32[]{:S(2)}) collective-permute-start(f32[2,2,292,18]{2,1,3,0:T(2,128)S(1)} %copy.19), channel_id=1, source_target_pairs={{0,8},{8,16},{16,24},{24,0},{1,9},{9,17},{17,25},{25,1},{2,10},{10... | collective-permute-start | bytes 252296 | tf_op jit(solution)/shard_map/ppermute | solution.py:28
  72.3 0.8 copy.24.lon_col
  73.1 4.5 %collective-permute-done.11 = f32[2,2,292,18]{2,1,3,0:T(2,128)S(1)} collective-permute-done((f32[2,2,292,18]{2,1,3,0:T(2,128)S(1)}, f32[2,2,292,18]{2,1,3,0:T(2,128)S(1)}, u32[]{:S(2)}, u32[]{:S(2)}) %collective-permute-start.11) | collective-permute-done | bytes 84128 | tf_op jit(solution)/shard_map/ppermute | solution.py:28
  78.2 1.0 add.78
  79.3 2.9 %collective-permute-start.6 = (f32[2,128,10]{2,1,0:T(8,128)S(1)}, f32[2,128,10]{2,1,0:T(8,128)S(1)}, u32[]{:S(2)}, u32[]{:S(2)}) collective-permute-start(f32[2,128,10]{2,1,0:T(8,128)S(1)} %get-tuple-element.25), channel_id=1, source_target_pairs={{8,0},{16,8},{24,16},{0,24},{9,1},{17,9},{25,17},{1,25},{10,2},{18... | collective-permute-start | bytes 30728 | tf_op jit(solution)/shard_map/ppermute | solution.py:29
  82.2 5.5 %shard_map.107 = (bf16[5,144,128]{2,1,0:T(8,128)(2,1)}, bf16[5,144,128]{2,1,0:T(8,128)(2,1)}) custom-call(bf16[40,2,128,128]{3,2,1,0:T(8,128)(2,1)} %perts.3, bf16[40,2,8,128]{3,2,1,0:T(8,128)(2,1)} %collective-permute-done.17.north, bf16[40,2,8,128]{3,2,1,0:T(8,128)(2,1)} %collective-permute-done.18.south), custom_call_target="tpu_custom_call" | custom-call | flops 754974720 | bytes 2621440 | tf_op jit(solution)/shard_map/pallas_call | solution.py:131
  87.7 2.9 %collective-permute-start.20 = (bf16[5,144,128]{2,1,0:T(8,128)(2,1)}, bf16[5,144,128]{2,1,0:T(8,128)(2,1)S(1)}, u32[]{:S(2)}, u32[]{:S(2)}) collective-permute-start(bf16[5,144,128]{2,1,0:T(8,128)(2,1)} %get-tuple-element.12), channel_id=1, source_target_pairs={{8,0},{16,8},{24,16},{0,24},{9,1},{17,9},{25,17},{1,25},{10,2},{18... | collective-permute-start | bytes 552968 | tf_op jit(solution)/shard_map/ppermute | solution.py:29
  90.7 3.8 %collective-permute-start.7 = (f32[2,10,148]{2,1,0:T(8,128)S(1)}, f32[2,10,148]{2,1,0:T(8,128)S(1)}, u32[]{:S(2)}, u32[]{:S(2)}) collective-permute-start(f32[2,10,148]{2,1,0:T(8,128)S(1)} %get-tuple-element.22), channel_id=1, source_target_pairs={{0,2},{2,4},{4,6},{1,3},{3,5},{5,7},{8,10},{10,12},{12,14},{9,11},... | collective-permute-start | bytes 35528 | tf_op jit(solution)/shard_map/ppermute | solution.py:28
  94.5 1.5 %collective-permute-start.8 = (f32[2,10,148]{2,1,0:T(8,128)S(1)}, f32[2,10,148]{2,1,0:T(8,128)S(1)}, u32[]{:S(2)}, u32[]{:S(2)}) collective-permute-start(f32[2,10,148]{2,1,0:T(8,128)S(1)} %get-tuple-element.23), channel_id=1, source_target_pairs={{2,0},{4,2},{6,4},{3,1},{5,3},{7,5},{10,8},{12,10},{14,12},{11,9},... | collective-permute-start | bytes 35528 | tf_op jit(solution)/shard_map/ppermute | solution.py:29
  96.0 1.5 %pad_maximum_fusion.fine = f32[2,2,292,292]{3,2,1,0:T(8,128)} fusion(f32[2,2,292,18]{3,2,1,0:T(8,128)S(1)} %copy.22, f32[2,2,292,18]{3,2,1,0:T(8,128)S(1)} %copy.21, f32[2,2,18,256]{3,2,1,0:T(8,128)S(1)} %copy-done.5, f32[2,2,18,256]{3,2,1,0:T(8,128)S(1)} %copy-done.3, f32[1,2,256,256]{3,2,1,0:T(8,128)S(1)} %bitcast.12, f32[1,2,256,256]{3,2,1,0:T(8,128)S(1)} %bitcast.15), kind=kLoop, calls=%fused_computation.24 | loop fusion | flops 1705280 | bytes 2728448 | tf_op jit(solution)/shard_map/concatenate | solution.py:41
  97.5 2.8 %collective-permute-done.8 = f32[2,10,148]{2,1,0:T(8,128)S(1)} collective-permute-done((f32[2,10,148]{2,1,0:T(8,128)S(1)}, f32[2,10,148]{2,1,0:T(8,128)S(1)}, u32[]{:S(2)}, u32[]{:S(2)}) %collective-permute-start.8) | collective-permute-done | bytes 11872 | tf_op jit(solution)/shard_map/ppermute | solution.py:29
  100.3 0.8 pad_maximum_fusion.2.coarse
  101.1 7.8 %shard_map.106 = (f32[2,256,256]{2,1,0:T(8,128)}, f32[2,144,256]{2,1,0:T(8,128)}) custom-call(f32[2,148,148]{2,1,0:T(8,128)} %pad_maximum_fusion.2.coarse, f32[2,2,292,292]{3,2,1,0:T(8,128)} %pad_maximum_fusion.fine, f32[292,2]{1,0:T(8,128)} %copy.23.lat_col, f32[2,292]{1,0:T(2,128)} %get-tuple-element.28.lat_row, f32[292,2]{1,0:T(8,128)} %copy.24.lon_col, ...), custom_call_target="tpu_custom_call" | custom-call | flops 536870912 | bytes 2097152 | tf_op jit(solution)/shard_map/pallas_call | solution.py:287
  109.7 23.7 %shard_map.108 = f32[40,2,128,128]{3,2,1,0:T(8,128)} custom-call(bf16[40,2,128,128]{3,2,1,0:T(8,128)(2,1)} %alpha.3, bf16[40,2,128,128]{3,2,1,0:T(8,128)(2,1)} %perts.3, bf16[40,2,8,128]{3,2,1,0:T(8,128)(2,1)} %collective-permute-done.17.north, bf16[40,2,8,128]{3,2,1,0:T(8,128)(2,1)} %collective-permute-done.18.south, bf16[5,144,128]{2,1,0:T(8,128)(2,1)} %copy-done.6, ...), custom_call_target="tpu_custom_call" | custom-call | flops 2684354560 | bytes 10485760 | tf_op jit(solution)/shard_map/pallas_call | solution.py:228
  (84 shorter events, 11.9 us)
Async XLA Ops:
  0.6 33.0 %copy-start.10 = (f32[256]{0:T(256)S(1)}, f32[256]{0:T(256)}, u32[]{:S(2)}) copy-start(f32[256]{0:T(256)} %param.13) | copy-start | bytes 3076
  0.6 35.6 %copy-start.11 = (f32[256]{0:T(256)S(1)}, f32[256]{0:T(256)}, u32[]{:S(2)}) copy-start(f32[256]{0:T(256)} %param.15) | copy-start | bytes 3076
  0.7 51.4 %copy-start = (f32[2,256,256]{2,1,0:T(8,128)S(1)}, f32[2,256,256]{2,1,0:T(8,128)}, u32[]{:S(2)}) copy-start(f32[2,256,256]{2,1,0:T(8,128)} %param.17) | copy-start | bytes 1572868
  0.7 51.4 %copy-start.1 = (f32[2,256,256]{2,1,0:T(8,128)S(1)}, f32[2,256,256]{2,1,0:T(8,128)}, u32[]{:S(2)}) copy-start(f32[2,256,256]{2,1,0:T(8,128)} %param.16) | copy-start | bytes 1572868
  2.2 25.5 %collective-permute-start.13 = (f32[2,18]{1,0:T(2,128)S(1)}, f32[2,18]{1,0:T(2,128)S(1)}, u32[]{:S(2)}, u32[]{:S(2)}) collective-permute-start(f32[2,18]{1,0:T(2,128)S(1)} %get-tuple-element.34), channel_id=1, source_target_pairs={{0,2},{2,4},{4,6},{1,3},{3,5},{5,7},{8,10},{10,12},{12,14},{9,11},... | collective-permute-start | bytes 440 | tf_op jit(solution)/shard_map/ppermute | solution.py:28
  7.1 21.9 %collective-permute-start.14 = (f32[2,18]{1,0:T(2,128)S(1)}, f32[2,18]{1,0:T(2,128)S(1)}, u32[]{:S(2)}, u32[]{:S(2)}) collective-permute-start(f32[2,18]{1,0:T(2,128)S(1)} %get-tuple-element.35), channel_id=1, source_target_pairs={{2,0},{4,2},{6,4},{3,1},{5,3},{7,5},{10,8},{12,10},{14,12},{11,9},... | collective-permute-start | bytes 440 | tf_op jit(solution)/shard_map/ppermute | solution.py:29
  9.9 23.8 %collective-permute-start.15 = (f32[2,18]{1,0:T(2,128)S(1)}, f32[2,18]{1,0:T(2,128)S(1)}, u32[]{:S(2)}, u32[]{:S(2)}) collective-permute-start(f32[2,18]{1,0:T(2,128)S(1)} %get-tuple-element.32), channel_id=1, source_target_pairs={{0,8},{8,16},{16,24},{24,0},{1,9},{9,17},{17,25},{25,1},{2,10},{10... | collective-permute-start | bytes 440 | tf_op jit(solution)/shard_map/ppermute | solution.py:28
  11.4 23.6 %collective-permute-start.16 = (f32[2,18]{1,0:T(2,128)S(1)}, f32[2,18]{1,0:T(2,128)S(1)}, u32[]{:S(2)}, u32[]{:S(2)}) collective-permute-start(f32[2,18]{1,0:T(2,128)S(1)} %get-tuple-element.33), channel_id=1, source_target_pairs={{8,0},{16,8},{24,16},{0,24},{9,1},{17,9},{25,17},{1,25},{10,2},{18... | collective-permute-start | bytes 440 | tf_op jit(solution)/shard_map/ppermute | solution.py:29
  13.7 32.5 %collective-permute-start.9 = (f32[2,2,18,256]{3,2,1,0:T(8,128)S(1)}, f32[2,2,18,256]{3,2,1,0:T(8,128)S(1)}, u32[]{:S(2)}, u32[]{:S(2)}) collective-permute-start(f32[2,2,18,256]{3,2,1,0:T(8,128)S(1)} %get-tuple-element.20), channel_id=1, source_target_pairs={{0,2},{2,4},{4,6},{1,3},{3,5},{5,7},{8,10},{10,12},{12,14},{9,11},... | collective-permute-start | bytes 221192 | tf_op jit(solution)/shard_map/ppermute | solution.py:28
  27.7 8.7 %collective-permute-start.1 = (bf16[40,2,8,128]{3,2,1,0:T(8,128)(2,1)S(1)}, bf16[40,2,8,128]{3,2,1,0:T(8,128)(2,1)S(1)}, u32[]{:S(2)}, u32[]{:S(2)}) collective-permute-start(bf16[40,2,8,128]{3,2,1,0:T(8,128)(2,1)S(1)} %get-tuple-element.16), channel_id=1, source_target_pairs={{2,0},{4,2},{6,4},{3,1},{5,3},{7,5},{10,8},{12,10},{14,12},{11,9},... | collective-permute-start | bytes 491528 | tf_op jit(solution)/shard_map/ppermute | solution.py:29
  29.0 7.4 %collective-permute-start = (bf16[40,2,8,128]{3,2,1,0:T(8,128)(2,1)S(1)}, bf16[40,2,8,128]{3,2,1,0:T(8,128)(2,1)S(1)}, u32[]{:S(2)}, u32[]{:S(2)}) collective-permute-start(bf16[40,2,8,128]{3,2,1,0:T(8,128)(2,1)S(1)} %get-tuple-element.17), channel_id=1, source_target_pairs={{0,2},{2,4},{4,6},{1,3},{3,5},{5,7},{8,10},{10,12},{12,14},{9,11},... | collective-permute-start | bytes 491528 | tf_op jit(solution)/shard_map/ppermute | solution.py:28
  33.7 18.3 %collective-permute-start.10 = (f32[2,2,18,256]{3,2,1,0:T(8,128)S(1)}, f32[2,2,18,256]{3,2,1,0:T(8,128)S(1)}, u32[]{:S(2)}, u32[]{:S(2)}) collective-permute-start(f32[2,2,18,256]{3,2,1,0:T(8,128)S(1)} %get-tuple-element.21), channel_id=1, source_target_pairs={{2,0},{4,2},{6,4},{3,1},{5,3},{7,5},{10,8},{12,10},{14,12},{11,9},... | collective-permute-start | bytes 221192 | tf_op jit(solution)/shard_map/ppermute | solution.py:29
  35.0 47.2 %collective-permute-start.18 = (bf16[40,2,8,128]{3,2,1,0:T(8,128)(2,1)}, bf16[40,2,8,128]{3,2,1,0:T(8,128)(2,1)}, u32[]{:S(2)}, u32[]{:S(2)}) collective-permute-start(bf16[40,2,8,128]{3,2,1,0:T(8,128)(2,1)} %get-tuple-element.14), channel_id=1, source_target_pairs={{2,0},{4,2},{6,4},{3,1},{5,3},{7,5},{10,8},{12,10},{14,12},{11,9},... | collective-permute-start | bytes 491528 | tf_op jit(solution)/shard_map/ppermute | solution.py:29
  43.2 9.0 %collective-permute-start.2 = (bf16[5,144,128]{2,1,0:T(8,128)(2,1)}, bf16[5,144,128]{2,1,0:T(8,128)(2,1)S(1)}, u32[]{:S(2)}, u32[]{:S(2)}) collective-permute-start(bf16[5,144,128]{2,1,0:T(8,128)(2,1)} %get-tuple-element.8), channel_id=1, source_target_pairs={{0,8},{8,16},{16,24},{24,0},{1,9},{9,17},{17,25},{25,1},{2,10},{10... | collective-permute-start | bytes 552968 | tf_op jit(solution)/shard_map/ppermute | solution.py:28
  43.8 8.9 %collective-permute-start.3 = (bf16[5,144,128]{2,1,0:T(8,128)(2,1)}, bf16[5,144,128]{2,1,0:T(8,128)(2,1)S(1)}, u32[]{:S(2)}, u32[]{:S(2)}) collective-permute-start(bf16[5,144,128]{2,1,0:T(8,128)(2,1)} %get-tuple-element.9), channel_id=1, source_target_pairs={{8,0},{16,8},{24,16},{0,24},{9,1},{17,9},{25,17},{1,25},{10,2},{18... | collective-permute-start | bytes 552968 | tf_op jit(solution)/shard_map/ppermute | solution.py:29
  46.2 21.8 %copy-start.2 = (f32[2,2,18,256]{3,2,1,0:T(8,128)}, f32[2,2,18,256]{3,2,1,0:T(8,128)S(1)}, u32[]{:S(2)}) copy-start(f32[2,2,18,256]{3,2,1,0:T(8,128)S(1)} %collective-permute-done.9) | copy-start | bytes 221188
  46.2 36.1 %collective-permute-start.17 = (bf16[40,2,8,128]{3,2,1,0:T(8,128)(2,1)}, bf16[40,2,8,128]{3,2,1,0:T(8,128)(2,1)}, u32[]{:S(2)}, u32[]{:S(2)}) collective-permute-start(bf16[40,2,8,128]{3,2,1,0:T(8,128)(2,1)} %get-tuple-element.15), channel_id=1, source_target_pairs={{0,2},{2,4},{4,6},{1,3},{3,5},{5,7},{8,10},{10,12},{12,14},{9,11},... | collective-permute-start | bytes 491528 | tf_op jit(solution)/shard_map/ppermute | solution.py:28
  52.0 15.9 %copy-start.4 = (f32[2,2,18,256]{3,2,1,0:T(8,128)}, f32[2,2,18,256]{3,2,1,0:T(8,128)S(1)}, u32[]{:S(2)}) copy-start(f32[2,2,18,256]{3,2,1,0:T(8,128)S(1)} %collective-permute-done.10) | copy-start | bytes 221188
  52.2 0.7 copy-start.12
  67.9 10.2 %collective-permute-start.4 = (f32[2,128,128]{2,1,0:T(8,128)}, f32[2,128,128]{2,1,0:T(8,128)}, u32[]{:S(2)}, u32[]{:S(2)}) collective-permute-start(f32[2,128,128]{2,1,0:T(8,128)} %shard_map.105), channel_id=1, source_target_pairs={{0,1},{1,0},{2,3},{3,2},{4,5},{5,4},{6,7},{7,6},{8,9},{9,8},{10,11... | collective-permute-start | bytes 393224 | tf_op jit(solution)/shard_map/ppermute | solution.py:340
  68.2 27.8 %copy-start.3 = (f32[2,2,18,256]{3,2,1,0:T(8,128)S(1)}, f32[2,2,18,256]{3,2,1,0:T(8,128)}, u32[]{:S(2)}) copy-start(f32[2,2,18,256]{3,2,1,0:T(8,128)} %copy-done.2) | copy-start | bytes 221188
  68.2 27.8 %copy-start.5 = (f32[2,2,18,256]{3,2,1,0:T(8,128)S(1)}, f32[2,2,18,256]{3,2,1,0:T(8,128)}, u32[]{:S(2)}) copy-start(f32[2,2,18,256]{3,2,1,0:T(8,128)} %copy-done.4) | copy-start | bytes 221188
  68.8 9.1 %collective-permute-start.12 = (f32[2,2,292,18]{2,1,3,0:T(2,128)S(1)}, f32[2,2,292,18]{2,1,3,0:T(2,128)S(1)}, u32[]{:S(2)}, u32[]{:S(2)}) collective-permute-start(f32[2,2,292,18]{2,1,3,0:T(2,128)S(1)} %copy.20), channel_id=1, source_target_pairs={{8,0},{16,8},{24,16},{0,24},{9,1},{17,9},{25,17},{1,25},{10,2},{18... | collective-permute-start | bytes 252296 | tf_op jit(solution)/shard_map/ppermute | solution.py:29
  69.5 8.1 %collective-permute-start.11 = (f32[2,2,292,18]{2,1,3,0:T(2,128)S(1)}, f32[2,2,292,18]{2,1,3,0:T(2,128)S(1)}, u32[]{:S(2)}, u32[]{:S(2)}) collective-permute-start(f32[2,2,292,18]{2,1,3,0:T(2,128)S(1)} %copy.19), channel_id=1, source_target_pairs={{0,8},{8,16},{16,24},{24,0},{1,9},{9,17},{17,25},{25,1},{2,10},{10... | collective-permute-start | bytes 252296 | tf_op jit(solution)/shard_map/ppermute | solution.py:28
  79.3 11.4 %collective-permute-start.5 = (f32[2,128,10]{2,1,0:T(8,128)S(1)}, f32[2,128,10]{2,1,0:T(8,128)S(1)}, u32[]{:S(2)}, u32[]{:S(2)}) collective-permute-start(f32[2,128,10]{2,1,0:T(8,128)S(1)} %get-tuple-element.24), channel_id=1, source_target_pairs={{0,8},{8,16},{16,24},{24,0},{1,9},{9,17},{17,25},{25,1},{2,10},{10... | collective-permute-start | bytes 30728 | tf_op jit(solution)/shard_map/ppermute | solution.py:28
  79.3 11.3 %collective-permute-start.6 = (f32[2,128,10]{2,1,0:T(8,128)S(1)}, f32[2,128,10]{2,1,0:T(8,128)S(1)}, u32[]{:S(2)}, u32[]{:S(2)}) collective-permute-start(f32[2,128,10]{2,1,0:T(8,128)S(1)} %get-tuple-element.25), channel_id=1, source_target_pairs={{8,0},{16,8},{24,16},{0,24},{9,1},{17,9},{25,17},{1,25},{10,2},{18... | collective-permute-start | bytes 30728 | tf_op jit(solution)/shard_map/ppermute | solution.py:29
  87.7 21.2 %collective-permute-start.19 = (bf16[5,144,128]{2,1,0:T(8,128)(2,1)}, bf16[5,144,128]{2,1,0:T(8,128)(2,1)S(1)}, u32[]{:S(2)}, u32[]{:S(2)}) collective-permute-start(bf16[5,144,128]{2,1,0:T(8,128)(2,1)} %get-tuple-element.11), channel_id=1, source_target_pairs={{0,8},{8,16},{16,24},{24,0},{1,9},{9,17},{17,25},{25,1},{2,10},{10... | collective-permute-start | bytes 552968 | tf_op jit(solution)/shard_map/ppermute | solution.py:28
  87.7 21.2 %collective-permute-start.20 = (bf16[5,144,128]{2,1,0:T(8,128)(2,1)}, bf16[5,144,128]{2,1,0:T(8,128)(2,1)S(1)}, u32[]{:S(2)}, u32[]{:S(2)}) collective-permute-start(bf16[5,144,128]{2,1,0:T(8,128)(2,1)} %get-tuple-element.12), channel_id=1, source_target_pairs={{8,0},{16,8},{24,16},{0,24},{9,1},{17,9},{25,17},{1,25},{10,2},{18... | collective-permute-start | bytes 552968 | tf_op jit(solution)/shard_map/ppermute | solution.py:29
  90.7 6.8 %collective-permute-start.7 = (f32[2,10,148]{2,1,0:T(8,128)S(1)}, f32[2,10,148]{2,1,0:T(8,128)S(1)}, u32[]{:S(2)}, u32[]{:S(2)}) collective-permute-start(f32[2,10,148]{2,1,0:T(8,128)S(1)} %get-tuple-element.22), channel_id=1, source_target_pairs={{0,2},{2,4},{4,6},{1,3},{3,5},{5,7},{8,10},{10,12},{12,14},{9,11},... | collective-permute-start | bytes 35528 | tf_op jit(solution)/shard_map/ppermute | solution.py:28
  94.5 5.8 %collective-permute-start.8 = (f32[2,10,148]{2,1,0:T(8,128)S(1)}, f32[2,10,148]{2,1,0:T(8,128)S(1)}, u32[]{:S(2)}, u32[]{:S(2)}) collective-permute-start(f32[2,10,148]{2,1,0:T(8,128)S(1)} %get-tuple-element.23), channel_id=1, source_target_pairs={{2,0},{4,2},{6,4},{3,1},{5,3},{7,5},{10,8},{12,10},{14,12},{11,9},... | collective-permute-start | bytes 35528 | tf_op jit(solution)/shard_map/ppermute | solution.py:29
  108.9 0.7 copy-start.6
  109.0 0.7 copy-start.7
  (3 other events, 2.0 us)

commit v2 on v1

--- a/solution.py
+++ b/solution.py
@@ -7,38 +7,14 @@
 
 HB = 8
 GROUP = 8
-CH = HB + 2
-FH = 2 * HB + 2
+FR = 24
+FC = 32
+CR = 16
+MESH = pl.DeviceIdType.MESH
+VMEM_LIMIT = 60 * 2**20
 HIGHEST = lax.Precision.HIGHEST
 F32 = jnp.float32
 BF16 = jnp.bfloat16
-
-
-def shifts(axis, periodic):
-    count = lax.axis_size(axis)
-    forward = [(i, i + 1) for i in range(count - 1)]
-    if periodic:
-        forward.append((count - 1, 0))
-    return forward, [(target, source) for source, target in forward]
-
-
-def swap_edges(low_edge, high_edge, axis, periodic):
-    forward, backward = shifts(axis, periodic)
-    return (
-        lax.ppermute(high_edge, axis, forward),
-        lax.ppermute(low_edge, axis, backward),
-    )
-
-
-def framed(block, axis, dim, width, periodic):
-    size = block.shape[dim]
-    low, high = swap_edges(
-        lax.slice_in_dim(block, 0, width, axis=dim),
-        lax.slice_in_dim(block, size - width, size, axis=dim),
-        axis,
-        periodic,
-    )
-    return jnp.concatenate([block, low, high], axis=dim)
 
 
 def place(order, size, width):
@@ -89,54 +65,227 @@
     return jnp.concatenate([north.astype(F32), south.astype(F32)], axis=0)
 
 
-def pack_kernel(core, north, south, right, left, pick):
-    cols = core.shape[3]
+class Link:
+    def __init__(self, axis, step, src, dst, send, recv, slot, periodic):
+        me, count = lax.axis_index(axis), lax.axis_size(axis)
+        target = me + step
+        self.sends = self.gets = None
+        if periodic:
+            target = lax.rem(target + count, count)
+        else:
+            self.sends = (target >= 0) & (target < count)
+            self.gets = (me - step >= 0) & (me - step < count)
+        self.dst = dst
+        self.copy = pltpu.make_async_remote_copy(
+            src_ref=src,
+            dst_ref=dst,
+            send_sem=send.at[slot],
+            recv_sem=recv.at[slot],
+            device_id={axis: target},
+            device_id_type=MESH,
+        )
+
+    def start(self):
+        if self.sends is None:
+            self.copy.start()
+        else:
+            pl.when(self.sends)(self.copy.start)
+
+    def arrive(self):
+        if self.gets is None:
+            self.copy.wait_recv()
+        else:
+            pl.when(self.gets)(self.copy.wait_recv)
+
+            @pl.when(jnp.logical_not(self.gets))
+            def _():
+                self.dst[...] = jnp.zeros_like(self.dst)
+
+    def sent(self):
+        if self.sends is None:
+            self.copy.wait_send()
+        else:
+            pl.when(self.sends)(self.copy.wait_send)
+
+
+def greet(others):
+    barrier = pltpu.get_barrier_semaphore()
+    gx, gxn = lax.axis_index("gx"), lax.axis_size("gx")
+    gy, gyn = lax.axis_index("gy"), lax.axis_size("gy")
+    for step in (1, gxn - 1):
+        pl.semaphore_signal(
+            barrier, inc=1, device_id={"gx": lax.rem(gx + step, gxn)}, device_id_type=MESH
+        )
+    for peer in others:
+        pl.semaphore_signal(barrier, inc=1, device_id={"ma": peer}, device_id_type=MESH)
+    for step, there in ((-1, gy > 0), (1, gy < gyn - 1)):
+
+        @pl.when(there)
+        def _(step=step):
+            pl.semaphore_signal(barrier, inc=1, device_id={"gy": gy + step}, device_id_type=MESH)
+
+    below, above = jnp.minimum(gy, 1), jnp.minimum(gyn - 1 - gy, 1)
+    pl.semaphore_wait(barrier, 2 + len(others) + below + above)
+
+
+def exchange_kernel(
+    alpha, perts, innov, weight, lat, lon,
+    a_north, a_south, a_west, a_east, p_north, p_south, p_west, p_east,
+    fine_low, fine_high, fine_west, fine_east, lat_low, lat_high, lon_west, lon_east,
+    a_tile, p_tile, fine_tile, pick, a_right, a_left, p_right, p_left, f_right, f_left,
+    send, recv, local,
+):
+    members, levels, rows, cols = alpha.shape
     half = GROUP * HB
-    levels = core.shape[1]
-
-    @pl.when(pl.program_id(0) == 0)
-    def _():
-        r = lax.broadcasted_iota(jnp.int32, (cols, 4 * half), 0)
-        c = lax.broadcasted_iota(jnp.int32, (cols, 4 * half), 1)
-        for l in range(levels):
-            for k in range(GROUP):
-                to_right = c - (l * half + HB * k)
-                to_left = c - 2 * half - ((1 - l) * half + HB * k)
-                hit = ((to_right >= 0) & (to_right < HB) & (r == cols - HB + to_right)) | (
-                    (to_left >= 0) & (to_left < HB) & (r == to_left)
-                )
-                pick[l * GROUP + k] = jnp.where(hit, 1.0, 0.0).astype(BF16)
-
-    total = None
+    frows, fcols = innov.shape[1:]
+    loads = [
+        pltpu.make_async_copy(src, dst, local.at[i])
+        for i, (src, dst) in enumerate(
+            ((alpha, a_tile), (perts, p_tile), (innov, fine_tile.at[0]), (weight, fine_tile.at[1]))
+        )
+    ]
+    for load in loads:
+        load.start()
+    greet(())
+    slots = iter(range(64))
+
+    def link(axis, step, src, dst):
+        return Link(axis, step, src, dst, send, recv, next(slots), axis == "gx")
+
+    a_rows = [
+        link("gy", 1, alpha.at[:, :, pl.ds(rows - HB, HB), :], a_north),
+        link("gy", -1, alpha.at[:, :, pl.ds(0, HB), :], a_south),
+    ]
+    f_rows = [
+        link("gy", 1, innov.at[:, pl.ds(frows - FR, FR), :], fine_low.at[0]),
+        link("gy", -1, innov.at[:, pl.ds(0, FR), :], fine_high.at[0]),
+        link("gy", 1, weight.at[:, pl.ds(frows - FR, FR), :], fine_low.at[1]),
+        link("gy", -1, weight.at[:, pl.ds(0, FR), :], fine_high.at[1]),
+    ]
+    p_rows = [
+        link("gy", 1, perts.at[:, :, pl.ds(rows - HB, HB), :], p_north),
+        link("gy", -1, perts.at[:, :, pl.ds(0, HB), :], p_south),
+    ]
+    small = [
+        link("gy", 1, lat, lat_low),
+        link("gy", -1, lat, lat_high),
+        link("gx", 1, lon, lon_west),
+        link("gx", -1, lon, lon_east),
+    ]
+    for one in a_rows + f_rows + p_rows + small:
+        one.start()
+
+    r = lax.broadcasted_iota(jnp.int32, (cols, 4 * half), 0)
+    c = lax.broadcasted_iota(jnp.int32, (cols, 4 * half), 1)
     for l in range(levels):
         for k in range(GROUP):
-            edge = rows16(north[k, l], south[k, l]).astype(BF16)
-            part = dot(jnp.concatenate([core[k, l], edge], axis=0), pick[l * GROUP + k])
-            total = part if total is None else total + part
-    right[0] = total[:, : 2 * half].astype(BF16)
-    left[0] = total[:, 2 * half :].astype(BF16)
+            to_right = c - (l * half + HB * k)
+            to_left = c - 2 * half - ((1 - l) * half + HB * k)
+            hit = ((to_right >= 0) & (to_right < HB) & (r == cols - HB + to_right)) | (
+                (to_left >= 0) & (to_left < HB) & (r == to_left)
+            )
+            pick[l * GROUP + k] = jnp.where(hit, 1.0, 0.0).astype(BF16)
+
+    def packed(first, count, right, left, piece):
+        @pl.loop(0, members // GROUP)
+        def _(g):
+            total = None
+            for l in range(levels):
+                for k in range(GROUP):
+                    part = dot(piece(g * GROUP + k, l), pick[l * GROUP + k])
+                    total = part if total is None else total + part
+            right[g, first : first + count] = total[:, : 2 * half].astype(BF16)
+            left[g, first : first + count] = total[:, 2 * half :].astype(BF16)
+
+    def sides(first, count, right, left, west, east):
+        span = pl.ds(first, count)
+        pair = [
+            link("gx", 1, right.at[:, span, :], west.at[:, span, :]),
+            link("gx", -1, left.at[:, span, :], east.at[:, span, :]),
+        ]
+        for one in pair:
+            one.start()
+        return pair
+
+    flying = []
+    fields = (
+        (a_tile, loads[0], a_rows, a_north, a_south, a_right, a_left, a_west, a_east),
+        (p_tile, loads[1], p_rows, p_north, p_south, p_right, p_left, p_west, p_east),
+    )
+    for tile, load, _, _, _, right, left, west, east in fields:
+        load.wait()
+        packed(0, rows, right, left, lambda m, l: tile[m, l])
+        flying += sides(0, rows, right, left, west, east)
+    for _, _, arrivals, north, south, right, left, west, east in fields:
+        for one in arrivals:
+            one.arrive()
+        packed(
+            rows, 2 * HB, right, left, lambda m, l: rows16(north[m, l], south[m, l]).astype(BF16)
+        )
+        flying += sides(rows, 2 * HB, right, left, west, east)
+    loads[2].wait()
+    loads[3].wait()
+    for one in f_rows:
+        one.arrive()
+
+    def edge_of(part, start):
+        return jnp.concatenate(
+            [part[i, l, :, start : start + FC] for i in range(2) for l in range(levels)], axis=1
+        )
+
+    for first, part in ((0, fine_tile), (frows, fine_low), (frows + FR, fine_high)):
+        count = part.shape[2]
+        f_right[first : first + count] = edge_of(part, fcols - FC)
+        f_left[first : first + count] = edge_of(part, 0)
+    f_sides = [link("gx", 1, f_right, fine_west), link("gx", -1, f_left, fine_east)]
+    for one in f_sides:
+        one.start()
+    for one in flying + f_sides + small:
+        one.arrive()
+    for one in a_rows + f_rows + p_rows + flying + f_sides + small:
+        one.sent()
 
 
 def cost(flops, nbytes):
     return pl.CostEstimate(flops=flops, bytes_accessed=nbytes, transcendentals=0)
 
 
-def pack(field, north, south):
-    members, levels, rows, cols = field.shape
-    steps = members // GROUP
-    tall = rows + 2 * HB
-    wide = 2 * GROUP * HB
-    strip = pl.BlockSpec((GROUP, levels, HB, cols), lambda g: (g, 0, 0, 0))
-    out = pl.BlockSpec((1, tall, wide), lambda g: (g, 0, 0))
+def exchange(alpha, perts, innov, weight, lat, lon):
+    members, levels, rows, cols = alpha.shape
+    steps, tall, wide = members // GROUP, rows + 2 * HB, 2 * GROUP * HB
+    frows, fcols = innov.shape[1:]
+    strip = (members, levels, HB, cols)
+    side = (steps, tall, wide)
+    fine_rows = (2, levels, FR, fcols)
+    fine_side = (frows + 2 * FR, 2 * levels * FC)
+    outs = [(strip, BF16)] * 2 + [(side, BF16)] * 2
+    outs = outs + outs + [(fine_rows, F32)] * 2 + [(fine_side, F32)] * 2
+    outs = outs + [(lat.shape, F32)] * 2 + [(lon.shape, F32)] * 2
+    vmem = pl.BlockSpec(memory_space=pltpu.VMEM)
+    anywhere = pl.BlockSpec(memory_space=pl.ANY)
     return pl.pallas_call(
-        pack_kernel,
-        grid=(steps,),
-        in_specs=[pl.BlockSpec((GROUP, levels, rows, cols), lambda g: (g, 0, 0, 0)), strip, strip],
-        out_specs=[out, out],
-        out_shape=[jax.ShapeDtypeStruct((steps, tall, wide), BF16)] * 2,
-        scratch_shapes=[pltpu.VMEM((levels * GROUP, cols, 2 * wide), BF16)],
-        cost_estimate=cost(members * levels * tall * cols * wide * 4, field.size * 2),
-    )(field, north, south)
+        exchange_kernel,
+        in_specs=[anywhere] * 4 + [vmem] * 2,
+        out_specs=[vmem] * len(outs),
+        out_shape=[jax.ShapeDtypeStruct(shape, kind) for shape, kind in outs],
+        scratch_shapes=[
+            pltpu.VMEM(alpha.shape, BF16),
+            pltpu.VMEM(alpha.shape, BF16),
+            pltpu.VMEM((2,) + innov.shape, F32),
+            pltpu.VMEM((levels * GROUP, cols, 2 * wide), BF16),
+        ]
+        + [pltpu.VMEM(side, BF16)] * 4
+        + [pltpu.VMEM(fine_side, F32)] * 2
+        + [
+            pltpu.SemaphoreType.DMA((24,)),
+            pltpu.SemaphoreType.DMA((24,)),
+            pltpu.SemaphoreType.DMA((4,)),
+        ],
+        compiler_params=pltpu.CompilerParams(
+            collective_id=0, has_side_effects=True, vmem_limit_bytes=VMEM_LIMIT
+        ),
+        cost_estimate=cost(2**30, 2**24),
+    )(alpha, perts, innov, weight, lat, lon)
 
 
 def merged(west, east, level):
@@ -249,57 +398,159 @@
     return jnp.dot(a, b, preferred_element_type=F32, precision=HIGHEST)
 
 
+def across(a, b, dims):
+    return lax.dot_general(
+        a, b, ((dims[:1], dims[1:]), ((), ())), precision=HIGHEST, preferred_element_type=F32
+    )
+
+
 def weigh(cell, index, weight):
-    return jnp.where(cell == index, 1.0 - weight, 0.0) + jnp.where(cell == index + 1, weight, 0.0)
-
-
-def fine_kernel(coarse, fine, lat_col, lat_row, lon_col, lon_row, increment, residual):
-    levels, rows, cols = coarse.shape[0], coarse.shape[1] - 2 * CH, coarse.shape[2] - 2 * CH
-    tall, wide = fine.shape[2], fine.shape[3]
+    cell = cell.astype(F32)
+    return jnp.where(cell == index, 1.0 - weight, 0.0) + jnp.where(cell == index + 1.0, weight, 0.0)
+
+
+def fine_kernel(
+    partial, innov, weight, fine_low, fine_high, fine_west, fine_east,
+    lat, lat_low, lat_high, lon, lon_west, lon_east,
+    increment, residual,
+    mine, other, cells, edge, low, high, send, recv,
+):
+    levels, rows, cols = partial.shape
+    frows, fcols = innov.shape[1:]
+    tall, wide = frows + 2 * FR, fcols + 2 * FC
     half = GROUP * HB
+    ma, count = lax.axis_index("ma"), lax.axis_size("ma")
+    peers = [lax.rem(ma + step, count) for step in range(1, count)]
+    greet(peers)
+    swaps = []
+    for i, peer in enumerate(peers):
+        swaps.append(
+            pltpu.make_async_remote_copy(
+                src_ref=partial,
+                dst_ref=other.at[i],
+                send_sem=send.at[i],
+                recv_sem=recv.at[i],
+                device_id={"ma": peer},
+                device_id_type=MESH,
+            )
+        )
+        swaps[-1].start()
 
     def iota(shape, dim):
         return lax.broadcasted_iota(jnp.int32, shape, dim)
 
-    def col(ref):
-        return ref[:, 0:1].astype(jnp.int32), ref[:, 1:2]
-
-    def row(ref):
-        return ref[0:1, :].astype(jnp.int32), ref[1:2, :]
-
-    up_lat = weigh(place(iota((tall, rows + 2 * CH), 1), rows, CH), *col(lat_col))
-    up_lon = weigh(place(iota((cols + 2 * CH, wide), 0), cols, CH), *row(lon_row))
-    down_lat = weigh(place(iota((rows + 2 * HB, tall), 0), rows, HB), *row(lat_row))
-    order = iota((wide, cols + 2 * half), 1)
-    q = order - cols
+    def along(own, before, after, width):
+        size = own.shape[1]
+        return jnp.concatenate(
+            [own[0:2], before[0:2, size - width : size], after[0:2, 0:width]], axis=1
+        )
+
+    lat_all = along(lat, lat_low, lat_high, FR)
+    lon_all = along(lon, lon_west, lon_east, FC)
+    lat_at = lat_all[0:1] - (lax.axis_index("gy") * rows).astype(F32)
+    lat_w = lat_all[1:2]
+    lon_total = float(cols * lax.axis_size("gx"))
+    lon_at = lon_all[0:1] - (lax.axis_index("gx") * cols).astype(F32)
+    lon_at = jnp.where(
+        lon_at < -64.0, lon_at + lon_total, jnp.where(lon_at >= lon_total - 64.0, lon_at - lon_total, lon_at)
+    )
+    lon_w = lon_all[1:2]
+    up_lat = weigh(place(iota((rows + 2 * CR, tall), 0), rows, CR), lat_at, lat_w)
+    down_lat = weigh(place(iota((rows + 2 * HB, tall), 0), rows, HB), lat_at, lat_w)
+
+    for copy in swaps:
+        copy.wait_recv()
     for l in range(levels):
-        inc = exact_dot(exact_dot(up_lat, coarse[l]), up_lon)
-        increment[l] = inc[: increment.shape[1], : increment.shape[2]]
-        misfit = fine[1, l] * (inc - fine[0, l])
-        west = (q // half) == l
-        pos = jnp.where(order < cols, order, jnp.where(west, q % HB - HB, cols + q % HB))
-        down_lon = weigh(pos, *col(lon_col))
-        residual[l] = exact_dot(down_lat, exact_dot(misfit, down_lon))
-
-
-def fine_step(coarse, fine, lat_data, lon_data, rows, cols, fine_rows, fine_cols):
-    levels = coarse.shape[0]
+        total = partial[l]
+        for i in range(count - 1):
+            total = total + other[i, l]
+        cells[l] = total
+        mine[:, 2 * l * FC : (2 * l + 1) * FC] = total[:, :FC]
+        mine[:, (2 * l + 1) * FC : (2 * l + 2) * FC] = total[:, cols - FC :]
+    base = count - 1
+    sides = [
+        Link("gx", 1, mine, cells.at[levels], send, recv, base, True),
+        Link("gx", -1, mine, cells.at[levels + 1], send, recv, base + 1, True),
+    ]
+    for one in sides:
+        one.start()
+    for one in sides:
+        one.arrive()
+    edge[0] = cells[:, rows - CR :, :]
+    edge[1] = cells[:, :CR, :]
+    ends = [
+        Link("gy", 1, edge.at[0], low, send, recv, base + 2, False),
+        Link("gy", -1, edge.at[1], high, send, recv, base + 3, False),
+    ]
+    for one in ends:
+        one.start()
+    for one in ends:
+        one.arrive()
+
+    def framed(i):
+        return jnp.concatenate([cells[i], low[i], high[i]], axis=0)
+
+    wings = [framed(levels), framed(levels + 1)]
+
+    def fine_of(i, core, l):
+        off = (i * levels + l) * FC
+        body_rows = jnp.concatenate([core[l], fine_low[i, l], fine_high[i, l]], axis=0)
+        return jnp.concatenate(
+            [body_rows, fine_west[:, off : off + FC], fine_east[:, off : off + FC]], axis=1
+        )
+
+    for l in range(levels):
+        order = iota((cols + 4 * levels * FC, wide), 0)
+        j = order - cols
+        lane = j % (2 * FC)
+        whose = (j % (2 * levels * FC)) // (2 * FC) == l
+        west = j < 2 * levels * FC
+        pos = jnp.where(west, lane - 2 * FC, cols + lane)
+        good = whose & ((west & (lane >= FC)) | ((j >= 2 * levels * FC) & (lane < FC)))
+        pos = jnp.where(order < cols, order, jnp.where(good, pos, -1000))
+        up_lon = weigh(pos, lon_at, lon_w)
+        wide_cells = jnp.concatenate([framed(l)] + wings, axis=1)
+        inc = across(up_lat, exact_dot(wide_cells, up_lon), (0, 0))
+        increment[l] = inc[:frows, :fcols]
+        misfit = fine_of(1, weight, l) * (inc - fine_of(0, innov, l))
+        order = iota((cols + 2 * half, wide), 0)
+        q = order - cols
+        pos = jnp.where(q // half == l, q % HB - HB, cols + q % HB)
+        down_lon = weigh(jnp.where(order < cols, order, pos), lon_at, lon_w)
+        residual[l] = exact_dot(down_lat, across(misfit, down_lon, (1, 1)))
+    for copy in swaps:
+        copy.wait_send()
+    for one in sides + ends:
+        one.sent()
+
+
+def fine_step(partial, innov, weight, fine_halos, lat, lat_halos, lon, lon_halos):
+    levels, rows, cols = partial.shape
+    others = lax.axis_size("ma") - 1
+    vmem = pl.BlockSpec(memory_space=pltpu.VMEM)
     return pl.pallas_call(
         fine_kernel,
+        in_specs=[vmem] * 13,
+        out_specs=[vmem] * 2,
         out_shape=[
-            jax.ShapeDtypeStruct((levels, fine_rows, fine_cols), F32),
+            jax.ShapeDtypeStruct(innov.shape, F32),
             jax.ShapeDtypeStruct((levels, rows + 2 * HB, cols + 2 * GROUP * HB), F32),
         ],
+        scratch_shapes=[
+            pltpu.VMEM((rows, 2 * levels * FC), F32),
+            pltpu.VMEM((others, levels, rows, cols), F32),
+            pltpu.VMEM((levels + 2, rows, cols), F32),
+            pltpu.VMEM((2, levels + 2, CR, cols), F32),
+            pltpu.VMEM((levels + 2, CR, cols), F32),
+            pltpu.VMEM((levels + 2, CR, cols), F32),
+            pltpu.SemaphoreType.DMA((others + 4,)),
+            pltpu.SemaphoreType.DMA((others + 4,)),
+        ],
+        compiler_params=pltpu.CompilerParams(
+            collective_id=1, has_side_effects=True, vmem_limit_bytes=VMEM_LIMIT
+        ),
         cost_estimate=cost(2**29, 2**21),
-    )(coarse, fine, lat_data.T, lat_data, lon_data.T, lon_data)
-
-
-def halo_fields(field):
-    rows = field.shape[2]
-    north, south = swap_edges(field[:, :, :HB], field[:, :, rows - HB :], "gy", False)
-    right, left = pack(field, north, south)
-    west, east = swap_edges(left, right, "gx", True)
-    return north, south, west, east
+    )(partial, innov, weight, *fine_halos, lat, *lat_halos, lon, *lon_halos)
 
 
 def body(
@@ -315,33 +566,16 @@
 ):
     rows, cols = alpha_fields.shape[2:]
     lon, lat = filter_matrices(band_widths, rows, cols)
-    a_north, a_south, a_west, a_east = halo_fields(alpha_fields)
-    p_north, p_south, p_west, p_east = halo_fields(member_perts)
-
-    fine = jnp.stack([innovation, obs_weight])
-    fine = framed(framed(fine, "gy", 2, FH, False), "gx", 3, FH, True)
-    lat_start = lax.axis_index("gy") * rows
-    lon_start = lax.axis_index("gx") * cols
-    lon_total = cols * lax.axis_size("gx")
-    lat_data = framed(jnp.stack([lat_index.astype(F32), lat_weight]), "gy", 1, FH, False)
-    lon_data = framed(jnp.stack([lon_index.astype(F32), lon_weight]), "gx", 1, FH, True)
-    lat_rel = lat_data[0] - lat_start.astype(F32)
-    lon_rel = (
-        jnp.remainder(lon_data[0].astype(jnp.int32) - lon_start + CH, lon_total) - CH
-    ).astype(F32)
-    lat_data = jnp.stack([lat_rel, lat_data[1]])
-    lon_data = jnp.stack([lon_rel, lon_data[1]])
-
+    def table(index, weight):
+        blank = jnp.zeros((6,) + index.shape, F32)
+        return jnp.concatenate([index.astype(F32)[None], weight[None], blank])
+
+    lat_data, lon_data = table(lat_index, lat_weight), table(lon_index, lon_weight)
+    halos = exchange(alpha_fields, member_perts, innovation, obs_weight, lat_data, lon_data)
+    a_north, a_south, a_west, a_east, p_north, p_south, p_west, p_east = halos[:8]
     partial = forward(alpha_fields, a_north, a_south, a_west, a_east, member_perts, lon, lat)
-    count = lax.axis_size("ma")
-    total = partial
-    moving = partial
-    for _ in range(count - 1):
-        moving = lax.ppermute(moving, "ma", [(i, (i + 1) % count) for i in range(count)])
-        total = total + moving
-    coarse = framed(framed(total, "gx", 2, CH, True), "gy", 1, CH, False)
     increment, residual = fine_step(
-        coarse, fine, lat_data, lon_data, rows, cols, innovation.shape[1], innovation.shape[2]
+        partial, innovation, obs_weight, halos[8:12], lat_data, halos[12:14], lon_data, halos[14:16]
     )
     gradient = adjoint(
         alpha_fields, member_perts, p_north, p_south, p_west, p_east, residual, lon, lat

time: 134 us -> 101 us (0.75)
  starting transfers between devices: 44.2 us -> 0 us
  Pallas kernels: 56.9 us -> 89.5 us
  waiting for transfers between devices: 7.96 us -> 0 us
  local copies, waits for them, and re-layouts: 8.65 us -> 0.88 us
  other arithmetic: 14.7 us -> 9.33 us
    ppermute x21 -> x0, starting transfers between devices: 44.2 us -> none  [the longest x10 27.2 us: swap_edges(): lax.ppermute(high_edge, axis, forward)]
    pallas_call x3 -> x2, Pallas kernels: 18.8 us -> 51.3 us  [the longest x1 32.5 us: exchange(): pl.pallas_call(exchange_kernel, in_specs=[anywhere] * 4 + [vmem] * 2, out...]
    ppermute x21 -> x0, waiting for transfers between devices: 7.96 us -> none  [the longest x10 4.56 us: swap_edges(): lax.ppermute(high_edge, axis, forward)]
    slice x7 -> x0, local copies, waits for them, and re-layouts: 3.66 us -> none  [the longest x2 2.81 us: halo_fields(): field[:, :, :HB]]
    another operation x3 -> x0, other arithmetic: 2.09 us -> none  [the longest x1 0.74 us: body(): jnp.stack([lat_index.astype(F32), lat_weight])]
    unnamed x28 -> x3, local copies, waits for them, and re-layouts: 2.87 us -> 0.8 us
    transpose x2 -> x0, local copies, waits for them, and re-layouts: 1.63 us -> none  [fine_step(): return pl.pallas_call(fine_kernel, out_shape=[jax.ShapeDtypeStruct((level...]
  transfers between devices with their start and end apart: 21 -> 0, of which waited for: 3 -> 0; matrix products, arithmetic and copies ran while one was open for 14% -> 0% of each run, Pallas kernels for 25% -> 0%
where the time goes in v2:
time: 101 us; the launch traced here: 100 us
  Pallas kernels  89.5 us (89%)
  other arithmetic  9.33 us (9%)
    pallas_call x1, Pallas kernels, exchange(): pl.pallas_call(exchange_kernel, in_specs=[anywhere] * 4 + [vmem] * 2, out...  32.5 us
    pallas_call x1, Pallas kernels, adjoint(): pl.pallas_call(adjoint_kernel, grid=(members // GROUP,), in_specs=[block,...  23.8 us
    pallas_call x1, Pallas kernels, fine_step(): pl.pallas_call(fine_kernel, in_specs=[vmem] * 13, out_specs=[vmem] * 2, o...  18.8 us
    pallas_call x1, Pallas kernels, forward(): pl.pallas_call(forward_kernel, grid=(members // GROUP,), in_specs=[block,...  14.4 us
    convert_element_type x2, other arithmetic, split_cols(): return jnp.where(column < half, high, value - high).astype(BF16)  5.66 us

profile of v2, /device:TPU:0, one launch (start us, length us, event | category | flops | bytes accessed | tf_op | source)
XLA Modules:
  0.0 100.4 jit_solution(2635350841022450498)
XLA Ops:
  0.6 0.7 multiply_multiply_fusion
  1.3 0.1 pad.5.clone
  1.4 0.2 fusion.14
  1.6 0.7 convert_element_type.28
  2.3 0.7 convert_element_type.29
  3.1 1.4 %maximum_maximum_fusion.1 = (f32[8,256]{1,0:T(8,128)}, f32[8,256]{1,0:T(8,128)}) fusion(f32[1,256]{1,0:T(1,128)} %bitcast.6, f32[1,256]{1,0:T(1,128)S(1)} %bitcast.5, f32[8]{0:T(128)S(1)} %pad.5.clone, f32[1,256]{1,0:T(1,128)} %bitcast.7, f32[1,256]{1,0:T(1,128)S(1)} %bitcast.4), kind=kLoop, calls=%fused_computation.28 | loop fusion | flops 8192 | bytes 20512 | tf_op jit(solution)/shard_map/concatenate | solution.py:571
  4.4 1.1 %fusion.12.lat = bf16[2,256,144]{2,1,0:T(8,128)(2,1)} fusion(f32[2]{0:T(128)S(1)} %sqrt.3, f32[2]{0:T(128)S(1)} %multiply_multiply_fusion, s32[256]{0:T(256)S(1)} %get-tuple-element.47, s32[256]{0:T(256)S(1)} %get-tuple-element.48, s32[144]{0:T(256)S(1)} %get-tuple-element.52, s32[144]{0:T(256)S(1)} %get-tuple-element.53, ...), kind=kLoop, calls=%fused_computation.25 | loop fusion | flops 1179648 | bytes 151472 | tf_op jit(solution)/shard_map/convert_element_type | solution.py:31
  5.6 32.5 %shard_map.104 = (bf16[40,2,8,128]{3,2,1,0:T(8,128)(2,1)}, bf16[40,2,8,128]{3,2,1,0:T(8,128)(2,1)}, bf16[5,144,128]{2,1,0:T(8,128)(2,1)}, bf16[5,144,128]{2,1,0:...) custom-call(bf16[40,2,128,128]{3,2,1,0:T(8,128)(2,1)} %alpha.5, ...), custom_call_target="tpu_custom_call" | custom-call | flops 1073741824 | bytes 16777216 | tf_op jit(solution)/shard_map/pallas_call | solution.py:266
  38.0 4.5 %fusion.6.lon = bf16[2,8,256,256]{3,2,1,0:T(8,128)(2,1)} fusion(f32[2]{0:T(128)S(1)} %sqrt.3, f32[2]{0:T(128)S(1)} %multiply_multiply_fusion, s32[256]{0:T(256)S(1)} %get-tuple-element.47, s32[256]{0:T(256)S(1)} %get-tuple-element.48, s32[256]{0:T(256)S(1)} %get-tuple-element.44, s32[256]{0:T(256)S(1)} %get-tuple-element.49, s32[256]{0:T(256)S(1)} %get-tuple-element.45, ...), kind=kLoop, calls=%fused_computation.16 | loop fusion | flops 41943040 | bytes 2106640 | tf_op jit(solution)/shard_map/convert_element_type | solution.py:31
  42.6 14.4 %shard_map.105.partial = f32[2,128,128]{2,1,0:T(8,128)} custom-call(bf16[40,2,128,128]{3,2,1,0:T(8,128)(2,1)} %alpha.5, bf16[40,2,8,128]{3,2,1,0:T(8,128)(2,1)} %get-tuple-element.20.north, bf16[40,2,8,128]{3,2,1,0:T(8,128)(2,1)} %get-tuple-element.21.south, bf16[5,144,128]{2,1,0:T(8,128)(2,1)} %get-tuple-element.22.west, ...), custom_call_target="tpu_custom_call" | custom-call | flops 2684354560 | bytes 5242880 | tf_op jit(solution)/shard_map/pallas_call | solution.py:364
  57.0 18.8 %shard_map.106 = (f32[2,256,256]{2,1,0:T(8,128)}, f32[2,144,256]{2,1,0:T(8,128)}) custom-call(f32[2,128,128]{2,1,0:T(8,128)} %shard_map.105.partial, f32[2,256,256]{2,1,0:T(8,128)} %innov.3, f32[2,256,256]{2,1,0:T(8,128)} %weight.3, f32[2,2,24,256]{3,2,1,0:T(8,128)} %get-tuple-element.24.fine_low, f32[2,2,24,256]{3,2,1,0:T(8,128)} %get-tuple-element.25.fine_high, ...), custom_call_target="tpu_custom_call" | custom-call | flops 536870912 | bytes 2097152 | tf_op jit(solution)/shard_map/pallas_call | solution.py:531
  75.8 0.0 copy-start
  75.8 23.8 %shard_map.107 = f32[40,2,128,128]{3,2,1,0:T(8,128)} custom-call(bf16[40,2,128,128]{3,2,1,0:T(8,128)(2,1)} %alpha.5, bf16[40,2,128,128]{3,2,1,0:T(8,128)(2,1)} %perts.5, bf16[40,2,8,128]{3,2,1,0:T(8,128)(2,1)} %get-tuple-element.33.north, bf16[40,2,8,128]{3,2,1,0:T(8,128)(2,1)} %get-tuple-element.34.south, bf16[5,144,128]{2,1,0:T(8,128)(2,1)} %get-tuple-element.35.west, ...), custom_call_target="tpu_custom_call" | custom-call | flops 2684354560 | bytes 10485760 | tf_op jit(solution)/shard_map/pallas_call | solution.py:377
  99.6 0.0 copy-done
  99.6 0.8 copy.12
  (12 shorter events, 0.1 us)
Async XLA Ops:
  75.8 23.8 %copy-start = (f32[2,256,256]{2,1,0:T(8,128)S(1)}, f32[2,256,256]{2,1,0:T(8,128)}, u32[]{:S(2)}) copy-start(f32[2,256,256]{2,1,0:T(8,128)} %get-tuple-element.58) | copy-start | bytes 1572868
